TPU v7x, 32 devices: a whole 2x2x4 slice. The times are simulated.
32 devices in a mesh: section: 4 (over y, core), row: 4 (over z), col: 2 (over x).
Axes of the slice: x: 2, y: 2, z: 4, core: 2. Of those that a mesh axis runs over, the one named last changes fastest.
Arguments:
- section_input: bfloat16 [4, 2, 32, 32, 128], P('section', None, 'row', 'col'), may hold values from -6 to 6
- first_pre: bfloat16 [4, 2, 32, 32, 128], P('section', None, 'row', 'col'), may hold values from -6 to 6
- second_pre: bfloat16 [4, 2, 32, 32, 128], P('section', None, 'row', 'col'), may hold values from -6 to 6
- out_grad: bfloat16 [2, 32, 32, 128], P(None, 'row', 'col'), may hold values from -6 to 6
- kernels: bfloat16 [4, 2, 3, 3, 128, 128], P('section'), may hold values from -0.1875 to 0.1875
- bn_scale: float32 [4, 2, 128], P('section'), may hold values from 0.5 to 2
- bn_shift: float32 [4, 2, 128], P('section'), may hold values from -3 to 3
Outputs:
- input_grad: bfloat16 [4, 2, 32, 32, 128], P('section', None, 'row', 'col')
- filter_grad: float32 [4, 2, 3, 3, 128, 128], P('section')
All inputs are finite; a program needn't handle non-finite values.
Results may differ from a plain program's by a relative error of at most 0.013.
Values may be sent and summed in bfloat16 or wider, within the bound.
A program may use at most 64 MiB of HBM per device.

v0:
```python
import jax
import jax.numpy as jnp
from jax import lax
from jax.sharding import PartitionSpec as P


def padded_2(cells, sides, width):
    for axis, dim in sides:
        count = lax.axis_size(axis)
        ends = count - 1
        head = lax.slice_in_dim(cells, 0, width, axis=dim)
        tail = lax.slice_in_dim(cells, cells.shape[dim] - width, cells.shape[dim], axis=dim)
        cells = jnp.concatenate(
            [
                lax.ppermute(tail, axis, [(i, (i + 1) % count) for i in range(ends)]),
                cells,
                lax.ppermute(head, axis, [((i + 1) % count, i) for i in range(ends)]),
            ],
            axis=dim,
        )
    return cells


def from_behind(value, axis, steps):
    count = lax.axis_size(axis)
    first, last = (max(0, -steps), min(count, count - steps))
    return lax.ppermute(value, axis, [(source, source + steps) for source in range(first, last)])


def correlate(padded, kernel):
    result = lax.conv_general_dilated(
        padded[None],
        kernel,
        (1, 1),
        "VALID",
        dimension_numbers=("NHWC", "HWIO", "NHWC"),
        preferred_element_type=jnp.float32,
    )
    return result[0]


def flip_kernel(kernel):
    return jnp.transpose(jnp.flip(kernel, (0, 1)), (0, 1, 3, 2))


def batched_kernel_grad(padded, gradient):
    rows_here, cols_here = (gradient.shape[1], gradient.shape[2])
    windows = jnp.stack(
        [
            padded[:, row_off : row_off + rows_here, col_off : col_off + cols_here]
            for row_off in range(3)
            for col_off in range(3)
        ]
    )
    summed = jnp.einsum("kmhwc,mhwd->kcd", windows, gradient, preferred_element_type=jnp.float32)
    return summed.reshape(3, 3, gradient.shape[3], gradient.shape[3])


def pick_micro(values, picked):
    return lax.dynamic_index_in_dim(values, picked, 0, keepdims=False)


def store_micro(buffer, value, picked, active):
    return jnp.where(active, lax.dynamic_update_index_in_dim(buffer, value, picked, 0), buffer)


def on_device(section_input, first_pre, second_pre, out_grad, kernels, bn_scale, bn_shift):
    section_index = lax.axis_index("section")
    sections = lax.axis_size("section")
    micros = out_grad.shape[0]
    rows_here, cols_here, width = (out_grad.shape[1], out_grad.shape[2], out_grad.shape[3])
    inputs_all = section_input[0]
    kernel = kernels[0]
    scales = bn_scale[0]
    shifts = bn_shift[0]
    first_norm_all = scales[0] * first_pre[0].astype(jnp.float32) + shifts[0]
    first_act_all = jnp.maximum(first_norm_all, 0.0).astype(jnp.bfloat16)
    second_norm_all = scales[1] * second_pre[0].astype(jnp.float32) + shifts[1]
    flip_first = flip_kernel(kernel[0])
    flip_second = flip_kernel(kernel[1])
    saved = padded_2(jnp.stack([inputs_all, first_act_all]), (("row", 2), ("col", 3)), 1)
    padded_inputs_all = saved[0]
    padded_act_all = saved[1]
    received = jnp.zeros(out_grad.shape[1:], jnp.bfloat16)
    outputs = jnp.zeros(out_grad.shape, jnp.bfloat16)
    first_grads = jnp.zeros(out_grad.shape, jnp.bfloat16)
    second_grads = jnp.zeros(out_grad.shape, jnp.bfloat16)
    for ticker in range(micros + sections - 1):
        micro_index = ticker - (sections - 1 - section_index)
        active = jnp.logical_and(micro_index >= 0, micro_index < micros)
        picked = jnp.clip(micro_index, 0, micros - 1)
        inputs = pick_micro(inputs_all, picked)
        first_norm = pick_micro(first_norm_all, picked)
        second_norm = pick_micro(second_norm_all, picked)
        incoming = jnp.where(section_index == sections - 1, pick_micro(out_grad, picked), received)
        masked = jnp.where(
            second_norm + inputs.astype(jnp.float32) > 0, incoming.astype(jnp.float32), 0.0
        )
        second_grad = (scales[1] * masked).astype(jnp.bfloat16)
        pad_second = padded_2(second_grad, (("row", 0), ("col", 1)), 1)
        act_grad = correlate(pad_second, flip_second)
        first_grad = (scales[0] * jnp.where(first_norm > 0, act_grad, 0.0)).astype(jnp.bfloat16)
        pad_first = padded_2(first_grad, (("row", 0), ("col", 1)), 1)
        input_grad = (masked + correlate(pad_first, flip_first)).astype(jnp.bfloat16)
        first_grads = store_micro(first_grads, first_grad, picked, active)
        second_grads = store_micro(second_grads, second_grad, picked, active)
        outputs = store_micro(outputs, input_grad, picked, active)
        if ticker + 2 < micros + sections:
            received = from_behind(input_grad, "section", -1)
    filter_acc = jnp.stack(
        [
            batched_kernel_grad(padded_inputs_all, first_grads),
            batched_kernel_grad(padded_act_all, second_grads),
        ]
    )
    pixels = micros * rows_here * lax.axis_size("row") * cols_here * lax.axis_size("col")
    factor = 1.0 / jnp.sqrt(jnp.float32(pixels))
    summed = lax.psum(filter_acc, ("row", "col"))
    return (outputs[None], (summed * factor)[None])


def solution(mesh):
    in_specs = (
        P("section", None, "row", "col", None),
        P("section", None, "row", "col", None),
        P("section", None, "row", "col", None),
        P(None, "row", "col", None),
        P("section", None, None, None, None, None),
        P("section", None, None),
        P("section", None, None),
    )
    out_specs = (P("section", None, "row", "col", None), P("section", None, None, None, None, None))
    return jax.shard_map(
        on_device, mesh=mesh, in_specs=in_specs, out_specs=out_specs, check_vma=False
    )
```

profile of v0, /device:TPU:0, one launch (start us, length us, event | category | flops | bytes accessed | tf_op | source)
XLA Modules:
  0.0 268.5 jit_solution(14341542754884638926)
XLA Ops:
  9.7 5.0 %collective-permute-start = (bf16[1,16,128]{2,1,0:T(8,128)(2,1)S(1)}, bf16[1,16,128]{2,1,0:T(8,128)(2,1)S(1)}, u32[]{:S(2)}, u32[]{:S(2)}) collective-permute-start(bf16[1,16,128]{2,1,0:T(8,128)(2,1)S(1)} %get-tuple-element.69), channel_id=1, source_target_pairs={{0,2},{2,4},{4,6},{1,3},{3,5},{5,7},{8,10},{10,12},{12,14},{9,11},... | collective-permute-start | bytes 12296 | tf_op jit(solution)/shard_map/ppermute | solution.py:15
  17.6 4.5 %collective-permute-start.44 = (bf16[2,2,1,16,128]{4,3,1,2,0:T(8,128)(2,1)S(1)}, bf16[2,2,1,16,128]{4,3,1,2,0:T(8,128)(2,1)S(1)}, u32[]{:S(2)}, u32[]{:S(2)}) collective-permute-start(bf16[2,2,1,16,128]{4,3,1,2,0:T(8,128)(2,1)S(1)} %get-tuple-element.28), channel_id=1, source_target_pairs={{0,2},{2,4},{4,6},{1,3},{3,5},{5,7},{8,10},{10,12},{12,14},{9,11},... | collective-permute-start | bytes 49160 | tf_op jit(solution)/shard_map/ppermute | solution.py:15
  23.5 3.4 %collective-permute-start.2 = (bf16[10,1,128]{2,1,0:T(2,128)(2,1)S(1)}, bf16[10,1,128]{2,1,0:T(2,128)(2,1)S(1)}, u32[]{:S(2)}, u32[]{:S(2)}) collective-permute-start(bf16[10,1,128]{2,1,0:T(2,128)(2,1)S(1)} %get-tuple-element.49), channel_id=1, source_target_pairs={{0,1},{2,3},{4,5},{6,7},{8,9},{10,11},{12,13},{14,15},{16,17},{18,... | collective-permute-start | bytes 7688 | tf_op jit(solution)/shard_map/ppermute | solution.py:15
  29.1 3.3 %collective-permute-done.3 = bf16[10,1,128]{2,1,0:T(2,128)(2,1)S(1)} collective-permute-done((bf16[10,1,128]{2,1,0:T(2,128)(2,1)S(1)}, bf16[10,1,128]{2,1,0:T(2,128)(2,1)S(1)}, u32[]{:S(2)}, u32[]{:S(2)}) %collective-permute-start.3) | collective-permute-done | bytes 2592 | tf_op jit(solution)/shard_map/ppermute | solution.py:17
  33.0 4.5 %collective-permute-start.4 = (bf16[1,16,128]{2,1,0:T(8,128)(2,1)S(1)}, bf16[1,16,128]{2,1,0:T(8,128)(2,1)S(1)}, u32[]{:S(2)}, u32[]{:S(2)}) collective-permute-start(bf16[1,16,128]{2,1,0:T(8,128)(2,1)S(1)} %get-tuple-element.67), channel_id=1, source_target_pairs={{0,2},{2,4},{4,6},{1,3},{3,5},{5,7},{8,10},{10,12},{12,14},{9,11},... | collective-permute-start | bytes 12296 | tf_op jit(solution)/shard_map/ppermute | solution.py:15
  38.9 4.1 %collective-permute-done.5 = bf16[1,16,128]{2,1,0:T(8,128)(2,1)S(1)} collective-permute-done((bf16[1,16,128]{2,1,0:T(8,128)(2,1)S(1)}, bf16[1,16,128]{2,1,0:T(8,128)(2,1)S(1)}, u32[]{:S(2)}, u32[]{:S(2)}) %collective-permute-start.5) | collective-permute-done | bytes 4128 | tf_op jit(solution)/shard_map/ppermute | solution.py:17
  46.1 4.1 %collective-permute-done.7 = bf16[10,1,128]{2,1,0:T(2,128)(2,1)S(1)} collective-permute-done((bf16[10,1,128]{2,1,0:T(2,128)(2,1)S(1)}, bf16[10,1,128]{2,1,0:T(2,128)(2,1)S(1)}, u32[]{:S(2)}, u32[]{:S(2)}) %collective-permute-start.7) | collective-permute-done | bytes 2592 | tf_op jit(solution)/shard_map/ppermute | solution.py:17
  55.0 3.0 %collective-permute-done.47 = bf16[2,2,10,1,128]{4,3,1,2,0:T(2,128)(2,1)S(1)} collective-permute-done((bf16[2,2,10,1,128]{4,3,1,2,0:T(2,128)(2,1)S(1)}, bf16[2,2,10,1,128]{4,3,1,2,0:T(2,128)(2,1)S(1)}, u32[]{:S(2)}, u32[]{:S(2)}) %collective-permute-start.47) | collective-permute-done | bytes 10272 | tf_op jit(solution)/shard_map/ppermute | solution.py:17
  58.5 3.5 %collective-permute-start.9 = (bf16[1,16,128]{2,1,0:T(8,128)(2,1)S(1)}, bf16[1,16,128]{2,1,0:T(8,128)(2,1)S(1)}, u32[]{:S(2)}, u32[]{:S(2)}) collective-permute-start(bf16[1,16,128]{2,1,0:T(8,128)(2,1)S(1)} %get-tuple-element.65), channel_id=1, source_target_pairs={{0,2},{2,4},{4,6},{1,3},{3,5},{5,7},{8,10},{10,12},{12,14},{9,11},... | collective-permute-start | bytes 12296 | tf_op jit(solution)/shard_map/ppermute | solution.py:15
  63.4 4.2 %collective-permute-done.10 = bf16[1,16,128]{2,1,0:T(8,128)(2,1)S(1)} collective-permute-done((bf16[1,16,128]{2,1,0:T(8,128)(2,1)S(1)}, bf16[1,16,128]{2,1,0:T(8,128)(2,1)S(1)}, u32[]{:S(2)}, u32[]{:S(2)}) %collective-permute-start.10) | collective-permute-done | bytes 4128 | tf_op jit(solution)/shard_map/ppermute | solution.py:17
  67.5 3.0 %collective-permute-start.11 = (bf16[10,1,128]{2,1,0:T(2,128)(2,1)S(1)}, bf16[10,1,128]{2,1,0:T(2,128)(2,1)S(1)}, u32[]{:S(2)}, u32[]{:S(2)}) collective-permute-start(bf16[10,1,128]{2,1,0:T(2,128)(2,1)S(1)} %get-tuple-element.45), channel_id=1, source_target_pairs={{0,1},{2,3},{4,5},{6,7},{8,9},{10,11},{12,13},{14,15},{16,17},{18,... | collective-permute-start | bytes 7688 | tf_op jit(solution)/shard_map/ppermute | solution.py:15
  71.8 4.2 %collective-permute-done.12 = bf16[10,1,128]{2,1,0:T(2,128)(2,1)S(1)} collective-permute-done((bf16[10,1,128]{2,1,0:T(2,128)(2,1)S(1)}, bf16[10,1,128]{2,1,0:T(2,128)(2,1)S(1)}, u32[]{:S(2)}, u32[]{:S(2)}) %collective-permute-start.12) | collective-permute-done | bytes 2592 | tf_op jit(solution)/shard_map/ppermute | solution.py:17
  76.5 3.5 %collective-permute-start.13 = (bf16[1,16,128]{2,1,0:T(8,128)(2,1)S(1)}, bf16[1,16,128]{2,1,0:T(8,128)(2,1)S(1)}, u32[]{:S(2)}, u32[]{:S(2)}) collective-permute-start(bf16[1,16,128]{2,1,0:T(8,128)(2,1)S(1)} %get-tuple-element.63), channel_id=1, source_target_pairs={{0,2},{2,4},{4,6},{1,3},{3,5},{5,7},{8,10},{10,12},{12,14},{9,11},... | collective-permute-start | bytes 12296 | tf_op jit(solution)/shard_map/ppermute | solution.py:15
  81.4 4.2 %collective-permute-done.14 = bf16[1,16,128]{2,1,0:T(8,128)(2,1)S(1)} collective-permute-done((bf16[1,16,128]{2,1,0:T(8,128)(2,1)S(1)}, bf16[1,16,128]{2,1,0:T(8,128)(2,1)S(1)}, u32[]{:S(2)}, u32[]{:S(2)}) %collective-permute-start.14) | collective-permute-done | bytes 4128 | tf_op jit(solution)/shard_map/ppermute | solution.py:17
  88.5 4.2 %collective-permute-done.16 = bf16[10,1,128]{2,1,0:T(2,128)(2,1)S(1)} collective-permute-done((bf16[10,1,128]{2,1,0:T(2,128)(2,1)S(1)}, bf16[10,1,128]{2,1,0:T(2,128)(2,1)S(1)}, u32[]{:S(2)}, u32[]{:S(2)}) %collective-permute-start.16) | collective-permute-done | bytes 2592 | tf_op jit(solution)/shard_map/ppermute | solution.py:17
  99.7 4.2 %collective-permute-done.19 = bf16[1,16,128]{2,1,0:T(8,128)(2,1)S(1)} collective-permute-done((bf16[1,16,128]{2,1,0:T(8,128)(2,1)S(1)}, bf16[1,16,128]{2,1,0:T(8,128)(2,1)S(1)}, u32[]{:S(2)}, u32[]{:S(2)}) %collective-permute-start.19) | collective-permute-done | bytes 4128 | tf_op jit(solution)/shard_map/ppermute | solution.py:17
  106.8 4.2 %collective-permute-done.21 = bf16[10,1,128]{2,1,0:T(2,128)(2,1)S(1)} collective-permute-done((bf16[10,1,128]{2,1,0:T(2,128)(2,1)S(1)}, bf16[10,1,128]{2,1,0:T(2,128)(2,1)S(1)}, u32[]{:S(2)}, u32[]{:S(2)}) %collective-permute-start.21) | collective-permute-done | bytes 2592 | tf_op jit(solution)/shard_map/ppermute | solution.py:17
  111.5 1.9 collective-permute-start.22
  114.8 4.2 %collective-permute-done.23 = bf16[1,16,128]{2,1,0:T(8,128)(2,1)S(1)} collective-permute-done((bf16[1,16,128]{2,1,0:T(8,128)(2,1)S(1)}, bf16[1,16,128]{2,1,0:T(8,128)(2,1)S(1)}, u32[]{:S(2)}, u32[]{:S(2)}) %collective-permute-start.23) | collective-permute-done | bytes 4128 | tf_op jit(solution)/shard_map/ppermute | solution.py:17
  122.0 4.2 %collective-permute-done.25 = bf16[10,1,128]{2,1,0:T(2,128)(2,1)S(1)} collective-permute-done((bf16[10,1,128]{2,1,0:T(2,128)(2,1)S(1)}, bf16[10,1,128]{2,1,0:T(2,128)(2,1)S(1)}, u32[]{:S(2)}, u32[]{:S(2)}) %collective-permute-start.25) | collective-permute-done | bytes 2592 | tf_op jit(solution)/shard_map/ppermute | solution.py:17
  133.1 4.2 %collective-permute-done.28 = bf16[1,16,128]{2,1,0:T(8,128)(2,1)S(1)} collective-permute-done((bf16[1,16,128]{2,1,0:T(8,128)(2,1)S(1)}, bf16[1,16,128]{2,1,0:T(8,128)(2,1)S(1)}, u32[]{:S(2)}, u32[]{:S(2)}) %collective-permute-start.28) | collective-permute-done | bytes 4128 | tf_op jit(solution)/shard_map/ppermute | solution.py:17
  140.3 4.2 %collective-permute-done.30 = bf16[10,1,128]{2,1,0:T(2,128)(2,1)S(1)} collective-permute-done((bf16[10,1,128]{2,1,0:T(2,128)(2,1)S(1)}, bf16[10,1,128]{2,1,0:T(2,128)(2,1)S(1)}, u32[]{:S(2)}, u32[]{:S(2)}) %collective-permute-start.30) | collective-permute-done | bytes 2592 | tf_op jit(solution)/shard_map/ppermute | solution.py:17
  145.0 1.9 collective-permute-start.31
  148.2 4.2 %collective-permute-done.32 = bf16[1,16,128]{2,1,0:T(8,128)(2,1)S(1)} collective-permute-done((bf16[1,16,128]{2,1,0:T(8,128)(2,1)S(1)}, bf16[1,16,128]{2,1,0:T(8,128)(2,1)S(1)}, u32[]{:S(2)}, u32[]{:S(2)}) %collective-permute-start.32) | collective-permute-done | bytes 4128 | tf_op jit(solution)/shard_map/ppermute | solution.py:17
  155.4 4.2 %collective-permute-done.34 = bf16[10,1,128]{2,1,0:T(2,128)(2,1)S(1)} collective-permute-done((bf16[10,1,128]{2,1,0:T(2,128)(2,1)S(1)}, bf16[10,1,128]{2,1,0:T(2,128)(2,1)S(1)}, u32[]{:S(2)}, u32[]{:S(2)}) %collective-permute-start.34) | collective-permute-done | bytes 2592 | tf_op jit(solution)/shard_map/ppermute | solution.py:17
  166.5 4.1 %collective-permute-done.37 = bf16[1,16,128]{2,1,0:T(8,128)(2,1)S(1)} collective-permute-done((bf16[1,16,128]{2,1,0:T(8,128)(2,1)S(1)}, bf16[1,16,128]{2,1,0:T(8,128)(2,1)S(1)}, u32[]{:S(2)}, u32[]{:S(2)}) %collective-permute-start.37) | collective-permute-done | bytes 4128 | tf_op jit(solution)/shard_map/ppermute | solution.py:17
  174.1 3.8 %collective-permute-done.39 = bf16[10,1,128]{2,1,0:T(2,128)(2,1)S(1)} collective-permute-done((bf16[10,1,128]{2,1,0:T(2,128)(2,1)S(1)}, bf16[10,1,128]{2,1,0:T(2,128)(2,1)S(1)}, u32[]{:S(2)}, u32[]{:S(2)}) %collective-permute-start.39) | collective-permute-done | bytes 2592 | tf_op jit(solution)/shard_map/ppermute | solution.py:17
  180.0 1.9 collective-permute-start.40
  183.2 4.2 %collective-permute-done.41 = bf16[1,16,128]{2,1,0:T(8,128)(2,1)S(1)} collective-permute-done((bf16[1,16,128]{2,1,0:T(8,128)(2,1)S(1)}, bf16[1,16,128]{2,1,0:T(8,128)(2,1)S(1)}, u32[]{:S(2)}, u32[]{:S(2)}) %collective-permute-start.41) | collective-permute-done | bytes 4128 | tf_op jit(solution)/shard_map/ppermute | solution.py:17
  190.4 4.2 %collective-permute-done.43 = bf16[10,1,128]{2,1,0:T(2,128)(2,1)S(1)} collective-permute-done((bf16[10,1,128]{2,1,0:T(2,128)(2,1)S(1)}, bf16[10,1,128]{2,1,0:T(2,128)(2,1)S(1)}, u32[]{:S(2)}, u32[]{:S(2)}) %collective-permute-start.43) | collective-permute-done | bytes 2592 | tf_op jit(solution)/shard_map/ppermute | solution.py:17
  195.1 64.2 %all-reduce.2.cloned.1.call-done = f32[2,3,3,128,128]{4,3,2,1,0:T(8,128)} async-done(((f32[2,3,3,128,128]{4,3,2,1,0:T(8,128)}), f32[2,3,3,128,128]{4,3,2,1,0:T(8,128)}) %all-reduce.2.cloned.1.call-update) | async-done | bytes 1179664 | tf_op jit(solution)/shard_map/psum | solution.py:118
  259.3 2.4 multiply_bitcast_fusion
  (232 shorter events, 72.3 us)
Async XLA Ops:
  7.2 252.1 %all-reduce.2.cloned.1.call-start = ((), (), s32[]{:S(2)}) async-start(), calls=%async_computation | async-start | bytes 2359296 | tf_op jit(solution)/shard_map/psum | solution.py:118
  9.7 13.8 %collective-permute-start = (bf16[1,16,128]{2,1,0:T(8,128)(2,1)S(1)}, bf16[1,16,128]{2,1,0:T(8,128)(2,1)S(1)}, u32[]{:S(2)}, u32[]{:S(2)}) collective-permute-start(bf16[1,16,128]{2,1,0:T(8,128)(2,1)S(1)} %get-tuple-element.69), channel_id=1, source_target_pairs={{0,2},{2,4},{4,6},{1,3},{3,5},{5,7},{8,10},{10,12},{12,14},{9,11},... | collective-permute-start | bytes 12296 | tf_op jit(solution)/shard_map/ppermute | solution.py:15
  14.7 8.8 %collective-permute-start.1 = (bf16[1,16,128]{2,1,0:T(8,128)(2,1)S(1)}, bf16[1,16,128]{2,1,0:T(8,128)(2,1)S(1)}, u32[]{:S(2)}, u32[]{:S(2)}) collective-permute-start(bf16[1,16,128]{2,1,0:T(8,128)(2,1)S(1)} %get-tuple-element.70), channel_id=1, source_target_pairs={{2,0},{4,2},{6,4},{3,1},{5,3},{7,5},{10,8},{12,10},{14,12},{11,9},... | collective-permute-start | bytes 12296 | tf_op jit(solution)/shard_map/ppermute | solution.py:17
  17.6 33.1 %collective-permute-start.44 = (bf16[2,2,1,16,128]{4,3,1,2,0:T(8,128)(2,1)S(1)}, bf16[2,2,1,16,128]{4,3,1,2,0:T(8,128)(2,1)S(1)}, u32[]{:S(2)}, u32[]{:S(2)}) collective-permute-start(bf16[2,2,1,16,128]{4,3,1,2,0:T(8,128)(2,1)S(1)} %get-tuple-element.28), channel_id=1, source_target_pairs={{0,2},{2,4},{4,6},{1,3},{3,5},{5,7},{8,10},{10,12},{12,14},{9,11},... | collective-permute-start | bytes 49160 | tf_op jit(solution)/shard_map/ppermute | solution.py:15
  22.2 28.5 %collective-permute-start.45 = (bf16[2,2,1,16,128]{4,3,1,2,0:T(8,128)(2,1)S(1)}, bf16[2,2,1,16,128]{4,3,1,2,0:T(8,128)(2,1)S(1)}, u32[]{:S(2)}, u32[]{:S(2)}) collective-permute-start(bf16[2,2,1,16,128]{4,3,1,2,0:T(8,128)(2,1)S(1)} %get-tuple-element.29), channel_id=1, source_target_pairs={{2,0},{4,2},{6,4},{3,1},{5,3},{7,5},{10,8},{12,10},{14,12},{11,9},... | collective-permute-start | bytes 49160 | tf_op jit(solution)/shard_map/ppermute | solution.py:17
  23.5 5.6 %collective-permute-start.2 = (bf16[10,1,128]{2,1,0:T(2,128)(2,1)S(1)}, bf16[10,1,128]{2,1,0:T(2,128)(2,1)S(1)}, u32[]{:S(2)}, u32[]{:S(2)}) collective-permute-start(bf16[10,1,128]{2,1,0:T(2,128)(2,1)S(1)} %get-tuple-element.49), channel_id=1, source_target_pairs={{0,1},{2,3},{4,5},{6,7},{8,9},{10,11},{12,13},{14,15},{16,17},{18,... | collective-permute-start | bytes 7688 | tf_op jit(solution)/shard_map/ppermute | solution.py:15
  26.9 5.5 %collective-permute-start.3 = (bf16[10,1,128]{2,1,0:T(2,128)(2,1)S(1)}, bf16[10,1,128]{2,1,0:T(2,128)(2,1)S(1)}, u32[]{:S(2)}, u32[]{:S(2)}) collective-permute-start(bf16[10,1,128]{2,1,0:T(2,128)(2,1)S(1)} %get-tuple-element.50), channel_id=1, source_target_pairs={{1,0},{3,2},{5,4},{7,6},{9,8},{11,10},{13,12},{15,14},{17,16},{19,... | collective-permute-start | bytes 7688 | tf_op jit(solution)/shard_map/ppermute | solution.py:17
  33.0 6.0 %collective-permute-start.4 = (bf16[1,16,128]{2,1,0:T(8,128)(2,1)S(1)}, bf16[1,16,128]{2,1,0:T(8,128)(2,1)S(1)}, u32[]{:S(2)}, u32[]{:S(2)}) collective-permute-start(bf16[1,16,128]{2,1,0:T(8,128)(2,1)S(1)} %get-tuple-element.67), channel_id=1, source_target_pairs={{0,2},{2,4},{4,6},{1,3},{3,5},{5,7},{8,10},{10,12},{12,14},{9,11},... | collective-permute-start | bytes 12296 | tf_op jit(solution)/shard_map/ppermute | solution.py:15
  37.5 5.5 %collective-permute-start.5 = (bf16[1,16,128]{2,1,0:T(8,128)(2,1)S(1)}, bf16[1,16,128]{2,1,0:T(8,128)(2,1)S(1)}, u32[]{:S(2)}, u32[]{:S(2)}) collective-permute-start(bf16[1,16,128]{2,1,0:T(8,128)(2,1)S(1)} %get-tuple-element.68), channel_id=1, source_target_pairs={{2,0},{4,2},{6,4},{3,1},{5,3},{7,5},{10,8},{12,10},{14,12},{11,9},... | collective-permute-start | bytes 12296 | tf_op jit(solution)/shard_map/ppermute | solution.py:17
  44.7 5.5 %collective-permute-start.7 = (bf16[10,1,128]{2,1,0:T(2,128)(2,1)S(1)}, bf16[10,1,128]{2,1,0:T(2,128)(2,1)S(1)}, u32[]{:S(2)}, u32[]{:S(2)}) collective-permute-start(bf16[10,1,128]{2,1,0:T(2,128)(2,1)S(1)} %get-tuple-element.48), channel_id=1, source_target_pairs={{1,0},{3,2},{5,4},{7,6},{9,8},{11,10},{13,12},{15,14},{17,16},{19,... | collective-permute-start | bytes 7688 | tf_op jit(solution)/shard_map/ppermute | solution.py:17
  50.7 4.3 %collective-permute-start.46 = (bf16[2,2,10,1,128]{4,3,1,2,0:T(2,128)(2,1)S(1)}, bf16[2,2,10,1,128]{4,3,1,2,0:T(2,128)(2,1)S(1)}, u32[]{:S(2)}, u32[]{:S(2)}) collective-permute-start(bf16[2,2,10,1,128]{4,3,1,2,0:T(2,128)(2,1)S(1)} %get-tuple-element.26), channel_id=1, source_target_pairs={{0,1},{2,3},{4,5},{6,7},{8,9},{10,11},{12,13},{14,15},{16,17},{18,... | collective-permute-start | bytes 30728 | tf_op jit(solution)/shard_map/ppermute | solution.py:15
  52.4 5.7 %collective-permute-start.47 = (bf16[2,2,10,1,128]{4,3,1,2,0:T(2,128)(2,1)S(1)}, bf16[2,2,10,1,128]{4,3,1,2,0:T(2,128)(2,1)S(1)}, u32[]{:S(2)}, u32[]{:S(2)}) collective-permute-start(bf16[2,2,10,1,128]{4,3,1,2,0:T(2,128)(2,1)S(1)} %get-tuple-element.27), channel_id=1, source_target_pairs={{1,0},{3,2},{5,4},{7,6},{9,8},{11,10},{13,12},{15,14},{17,16},{19,... | collective-permute-start | bytes 30728 | tf_op jit(solution)/shard_map/ppermute | solution.py:17
  53.7 4.7 %collective-permute-start.8 = (bf16[8,16,128]{2,1,0:T(8,128)(2,1)S(1)}, bf16[8,16,128]{2,1,0:T(8,128)(2,1)S(1)}, u32[]{:S(2)}, u32[]{:S(2)}) collective-permute-start(bf16[8,16,128]{2,1,0:T(8,128)(2,1)S(1)} %fusion.104), channel_id=1, source_target_pairs={{8,0},{16,8},{24,16},{9,1},{17,9},{25,17},{10,2},{18,10},{26,18},{... | collective-permute-start | bytes 98312 | tf_op jit(solution)/shard_map/ppermute | solution.py:27
  58.5 4.8 %collective-permute-start.9 = (bf16[1,16,128]{2,1,0:T(8,128)(2,1)S(1)}, bf16[1,16,128]{2,1,0:T(8,128)(2,1)S(1)}, u32[]{:S(2)}, u32[]{:S(2)}) collective-permute-start(bf16[1,16,128]{2,1,0:T(8,128)(2,1)S(1)} %get-tuple-element.65), channel_id=1, source_target_pairs={{0,2},{2,4},{4,6},{1,3},{3,5},{5,7},{8,10},{10,12},{12,14},{9,11},... | collective-permute-start | bytes 12296 | tf_op jit(solution)/shard_map/ppermute | solution.py:15
  62.0 5.5 %collective-permute-start.10 = (bf16[1,16,128]{2,1,0:T(8,128)(2,1)S(1)}, bf16[1,16,128]{2,1,0:T(8,128)(2,1)S(1)}, u32[]{:S(2)}, u32[]{:S(2)}) collective-permute-start(bf16[1,16,128]{2,1,0:T(8,128)(2,1)S(1)} %get-tuple-element.66), channel_id=1, source_target_pairs={{2,0},{4,2},{6,4},{3,1},{5,3},{7,5},{10,8},{12,10},{14,12},{11,9},... | collective-permute-start | bytes 12296 | tf_op jit(solution)/shard_map/ppermute | solution.py:17
  67.5 4.3 %collective-permute-start.11 = (bf16[10,1,128]{2,1,0:T(2,128)(2,1)S(1)}, bf16[10,1,128]{2,1,0:T(2,128)(2,1)S(1)}, u32[]{:S(2)}, u32[]{:S(2)}) collective-permute-start(bf16[10,1,128]{2,1,0:T(2,128)(2,1)S(1)} %get-tuple-element.45), channel_id=1, source_target_pairs={{0,1},{2,3},{4,5},{6,7},{8,9},{10,11},{12,13},{14,15},{16,17},{18,... | collective-permute-start | bytes 7688 | tf_op jit(solution)/shard_map/ppermute | solution.py:15
  70.5 5.5 %collective-permute-start.12 = (bf16[10,1,128]{2,1,0:T(2,128)(2,1)S(1)}, bf16[10,1,128]{2,1,0:T(2,128)(2,1)S(1)}, u32[]{:S(2)}, u32[]{:S(2)}) collective-permute-start(bf16[10,1,128]{2,1,0:T(2,128)(2,1)S(1)} %get-tuple-element.46), channel_id=1, source_target_pairs={{1,0},{3,2},{5,4},{7,6},{9,8},{11,10},{13,12},{15,14},{17,16},{19,... | collective-permute-start | bytes 7688 | tf_op jit(solution)/shard_map/ppermute | solution.py:17
  76.5 4.8 %collective-permute-start.13 = (bf16[1,16,128]{2,1,0:T(8,128)(2,1)S(1)}, bf16[1,16,128]{2,1,0:T(8,128)(2,1)S(1)}, u32[]{:S(2)}, u32[]{:S(2)}) collective-permute-start(bf16[1,16,128]{2,1,0:T(8,128)(2,1)S(1)} %get-tuple-element.63), channel_id=1, source_target_pairs={{0,2},{2,4},{4,6},{1,3},{3,5},{5,7},{8,10},{10,12},{12,14},{9,11},... | collective-permute-start | bytes 12296 | tf_op jit(solution)/shard_map/ppermute | solution.py:15
  80.0 5.5 %collective-permute-start.14 = (bf16[1,16,128]{2,1,0:T(8,128)(2,1)S(1)}, bf16[1,16,128]{2,1,0:T(8,128)(2,1)S(1)}, u32[]{:S(2)}, u32[]{:S(2)}) collective-permute-start(bf16[1,16,128]{2,1,0:T(8,128)(2,1)S(1)} %get-tuple-element.64), channel_id=1, source_target_pairs={{2,0},{4,2},{6,4},{3,1},{5,3},{7,5},{10,8},{12,10},{14,12},{11,9},... | collective-permute-start | bytes 12296 | tf_op jit(solution)/shard_map/ppermute | solution.py:17
  87.2 5.5 %collective-permute-start.16 = (bf16[10,1,128]{2,1,0:T(2,128)(2,1)S(1)}, bf16[10,1,128]{2,1,0:T(2,128)(2,1)S(1)}, u32[]{:S(2)}, u32[]{:S(2)}) collective-permute-start(bf16[10,1,128]{2,1,0:T(2,128)(2,1)S(1)} %get-tuple-element.44), channel_id=1, source_target_pairs={{1,0},{3,2},{5,4},{7,6},{9,8},{11,10},{13,12},{15,14},{17,16},{19,... | collective-permute-start | bytes 7688 | tf_op jit(solution)/shard_map/ppermute | solution.py:17
  98.3 5.5 %collective-permute-start.19 = (bf16[1,16,128]{2,1,0:T(8,128)(2,1)S(1)}, bf16[1,16,128]{2,1,0:T(8,128)(2,1)S(1)}, u32[]{:S(2)}, u32[]{:S(2)}) collective-permute-start(bf16[1,16,128]{2,1,0:T(8,128)(2,1)S(1)} %get-tuple-element.62), channel_id=1, source_target_pairs={{2,0},{4,2},{6,4},{3,1},{5,3},{7,5},{10,8},{12,10},{14,12},{11,9},... | collective-permute-start | bytes 12296 | tf_op jit(solution)/shard_map/ppermute | solution.py:17
  105.5 5.5 %collective-permute-start.21 = (bf16[10,1,128]{2,1,0:T(2,128)(2,1)S(1)}, bf16[10,1,128]{2,1,0:T(2,128)(2,1)S(1)}, u32[]{:S(2)}, u32[]{:S(2)}) collective-permute-start(bf16[10,1,128]{2,1,0:T(2,128)(2,1)S(1)} %get-tuple-element.42), channel_id=1, source_target_pairs={{1,0},{3,2},{5,4},{7,6},{9,8},{11,10},{13,12},{15,14},{17,16},{19,... | collective-permute-start | bytes 7688 | tf_op jit(solution)/shard_map/ppermute | solution.py:17
  113.5 5.5 %collective-permute-start.23 = (bf16[1,16,128]{2,1,0:T(8,128)(2,1)S(1)}, bf16[1,16,128]{2,1,0:T(8,128)(2,1)S(1)}, u32[]{:S(2)}, u32[]{:S(2)}) collective-permute-start(bf16[1,16,128]{2,1,0:T(8,128)(2,1)S(1)} %get-tuple-element.60), channel_id=1, source_target_pairs={{2,0},{4,2},{6,4},{3,1},{5,3},{7,5},{10,8},{12,10},{14,12},{11,9},... | collective-permute-start | bytes 12296 | tf_op jit(solution)/shard_map/ppermute | solution.py:17
  120.6 5.5 %collective-permute-start.25 = (bf16[10,1,128]{2,1,0:T(2,128)(2,1)S(1)}, bf16[10,1,128]{2,1,0:T(2,128)(2,1)S(1)}, u32[]{:S(2)}, u32[]{:S(2)}) collective-permute-start(bf16[10,1,128]{2,1,0:T(2,128)(2,1)S(1)} %get-tuple-element.40), channel_id=1, source_target_pairs={{1,0},{3,2},{5,4},{7,6},{9,8},{11,10},{13,12},{15,14},{17,16},{19,... | collective-permute-start | bytes 7688 | tf_op jit(solution)/shard_map/ppermute | solution.py:17
  131.8 5.5 %collective-permute-start.28 = (bf16[1,16,128]{2,1,0:T(8,128)(2,1)S(1)}, bf16[1,16,128]{2,1,0:T(8,128)(2,1)S(1)}, u32[]{:S(2)}, u32[]{:S(2)}) collective-permute-start(bf16[1,16,128]{2,1,0:T(8,128)(2,1)S(1)} %get-tuple-element.58), channel_id=1, source_target_pairs={{2,0},{4,2},{6,4},{3,1},{5,3},{7,5},{10,8},{12,10},{14,12},{11,9},... | collective-permute-start | bytes 12296 | tf_op jit(solution)/shard_map/ppermute | solution.py:17
  138.9 5.5 %collective-permute-start.30 = (bf16[10,1,128]{2,1,0:T(2,128)(2,1)S(1)}, bf16[10,1,128]{2,1,0:T(2,128)(2,1)S(1)}, u32[]{:S(2)}, u32[]{:S(2)}) collective-permute-start(bf16[10,1,128]{2,1,0:T(2,128)(2,1)S(1)} %get-tuple-element.38), channel_id=1, source_target_pairs={{1,0},{3,2},{5,4},{7,6},{9,8},{11,10},{13,12},{15,14},{17,16},{19,... | collective-permute-start | bytes 7688 | tf_op jit(solution)/shard_map/ppermute | solution.py:17
  146.9 5.5 %collective-permute-start.32 = (bf16[1,16,128]{2,1,0:T(8,128)(2,1)S(1)}, bf16[1,16,128]{2,1,0:T(8,128)(2,1)S(1)}, u32[]{:S(2)}, u32[]{:S(2)}) collective-permute-start(bf16[1,16,128]{2,1,0:T(8,128)(2,1)S(1)} %get-tuple-element.56), channel_id=1, source_target_pairs={{2,0},{4,2},{6,4},{3,1},{5,3},{7,5},{10,8},{12,10},{14,12},{11,9},... | collective-permute-start | bytes 12296 | tf_op jit(solution)/shard_map/ppermute | solution.py:17
  154.1 5.5 %collective-permute-start.34 = (bf16[10,1,128]{2,1,0:T(2,128)(2,1)S(1)}, bf16[10,1,128]{2,1,0:T(2,128)(2,1)S(1)}, u32[]{:S(2)}, u32[]{:S(2)}) collective-permute-start(bf16[10,1,128]{2,1,0:T(2,128)(2,1)S(1)} %get-tuple-element.36), channel_id=1, source_target_pairs={{1,0},{3,2},{5,4},{7,6},{9,8},{11,10},{13,12},{15,14},{17,16},{19,... | collective-permute-start | bytes 7688 | tf_op jit(solution)/shard_map/ppermute | solution.py:17
  165.2 5.5 %collective-permute-start.37 = (bf16[1,16,128]{2,1,0:T(8,128)(2,1)S(1)}, bf16[1,16,128]{2,1,0:T(8,128)(2,1)S(1)}, u32[]{:S(2)}, u32[]{:S(2)}) collective-permute-start(bf16[1,16,128]{2,1,0:T(8,128)(2,1)S(1)} %get-tuple-element.54), channel_id=1, source_target_pairs={{2,0},{4,2},{6,4},{3,1},{5,3},{7,5},{10,8},{12,10},{14,12},{11,9},... | collective-permute-start | bytes 12296 | tf_op jit(solution)/shard_map/ppermute | solution.py:17
  172.4 5.5 %collective-permute-start.39 = (bf16[10,1,128]{2,1,0:T(2,128)(2,1)S(1)}, bf16[10,1,128]{2,1,0:T(2,128)(2,1)S(1)}, u32[]{:S(2)}, u32[]{:S(2)}) collective-permute-start(bf16[10,1,128]{2,1,0:T(2,128)(2,1)S(1)} %get-tuple-element.34), channel_id=1, source_target_pairs={{1,0},{3,2},{5,4},{7,6},{9,8},{11,10},{13,12},{15,14},{17,16},{19,... | collective-permute-start | bytes 7688 | tf_op jit(solution)/shard_map/ppermute | solution.py:17
  181.9 5.5 %collective-permute-start.41 = (bf16[1,16,128]{2,1,0:T(8,128)(2,1)S(1)}, bf16[1,16,128]{2,1,0:T(8,128)(2,1)S(1)}, u32[]{:S(2)}, u32[]{:S(2)}) collective-permute-start(bf16[1,16,128]{2,1,0:T(8,128)(2,1)S(1)} %get-tuple-element.52), channel_id=1, source_target_pairs={{2,0},{4,2},{6,4},{3,1},{5,3},{7,5},{10,8},{12,10},{14,12},{11,9},... | collective-permute-start | bytes 12296 | tf_op jit(solution)/shard_map/ppermute | solution.py:17
  189.1 5.5 %collective-permute-start.43 = (bf16[10,1,128]{2,1,0:T(2,128)(2,1)S(1)}, bf16[10,1,128]{2,1,0:T(2,128)(2,1)S(1)}, u32[]{:S(2)}, u32[]{:S(2)}) collective-permute-start(bf16[10,1,128]{2,1,0:T(2,128)(2,1)S(1)} %get-tuple-element.32), channel_id=1, source_target_pairs={{1,0},{3,2},{5,4},{7,6},{9,8},{11,10},{13,12},{15,14},{17,16},{19,... | collective-permute-start | bytes 7688 | tf_op jit(solution)/shard_map/ppermute | solution.py:17
  (22 other events, 214.6 us)
Sparse Core Ops, SparseCore 0:
  180.0 79.2 all-reduce.1
where the time goes:
time: 270 us; the launch traced here: 269 us
  waiting for transfers between devices  150 us (56%)
  starting transfers between devices  87.4 us (32%)
  between operations  15.6 us (6%)
  other arithmetic  9.12 us (3%)
  matrix products  3.61 us (1%)
    ppermute x22, waiting for transfers between devices, padded_2(): lax.ppermute(head, axis, [((i + 1) % count, i) for i in range(ends)])  80.9 us
    psum x1, waiting for transfers between devices, on_device(): summed = lax.psum(filter_acc, ('row', 'col'))  64.2 us
    ppermute x22, starting transfers between devices, padded_2(): lax.ppermute(tail, axis, [(i, (i + 1) % count) for i in range(ends)])  53.8 us
    ppermute x22, starting transfers between devices, padded_2(): lax.ppermute(head, axis, [((i + 1) % count, i) for i in range(ends)])  28.4 us
  transfers between devices with their start and end apart: 49, of which 24 were waited for; matrix products, arithmetic and copies ran while one was open for 2% of the time, Pallas kernels for 0%

commit v1 on v0

v1 whole, which is shorter than its diff:
```python
import functools

import jax
import jax.numpy as jnp
from jax import lax
from jax.experimental import pallas as pl
from jax.experimental.pallas import tpu as pltpu
from jax.sharding import PartitionSpec as P

MESH = pl.DeviceIdType.MESH
SPREAD = [(dr, dc) for dr in (-1, 0, 1) for dc in (-1, 0, 1)]
F32 = jnp.float32
BF16 = jnp.bfloat16


def each(count, body):
    if count <= 16:
        for step in range(count):
            body(step)
    else:

        def run(step, carry):
            body(step)
            return carry

        lax.fori_loop(0, count, run, 0)


def kernel(
    dims, x_ref, p1_ref, p2_ref, og_ref, k_ref, scale_ref, shift_ref,
    out_ref, fg_ref,
    xf, p1f, p2f, gf, kt, c1, c2, cols1, cols2, act, red, inbox, final, gathered,
    halo_send, halo_recv, og_send, g_send, g_recv, rs_send, rs_recv, ag_send, ag_recv,
):
    axes, sections, rows_n, cols_n, factor = dims
    micros, rows, cols, width = x_ref.shape
    pitch = 2 * cols
    half = cols // 2
    group = rows_n * cols_n
    chunk = final.shape[0]
    s = lax.axis_index("section")
    r = lax.axis_index("row")
    c = lax.axis_index("col")
    me = r * cols_n + c

    def dev(sec, row, col):
        where = {"section": sec, "row": row, "col": col}
        return tuple(where[a] for a in axes)

    def inside(dr, dc):
        return (r + dr >= 0) & (r + dr < rows_n) & (c + dc >= 0) & (c + dc < cols_n)

    def src_part(dr, dc):
        row = {-1: pl.ds(0, 2), 0: pl.ds(0, rows), 1: pl.ds(rows - 2, 2)}[dr]
        col = {-1: pl.ds(0, half), 0: pl.ds(0, cols), 1: pl.ds(half, half)}[dc]
        return row, col

    def dst_part(dr, dc):
        row = {-1: pl.ds(rows + 2, 2), 0: pl.ds(2, rows), 1: pl.ds(0, 2)}[dr]
        col = {-1: pl.ds(cols, half), 0: pl.ds(0, cols), 1: pl.ds(cols + half, half)}[dc]
        return row, col

    def shift_copy(src, dst, m, dr, dc, send, recv, sec):
        a, b = src_part(dr, dc)
        p, q = dst_part(dr, dc)
        return pltpu.make_async_remote_copy(
            src_ref=src.at[m, a, b], dst_ref=dst.at[m, p, q],
            send_sem=send, recv_sem=recv,
            device_id=dev(sec, r + dr, c + dc), device_id_type=MESH,
        )

    for ref in (xf, p1f, p2f, gf):
        ref[...] = jnp.zeros(ref.shape, ref.dtype)

    barrier = pltpu.get_barrier_semaphore()

    def greet(step):
        peer = lax.rem(me + step + 1, group)
        pl.semaphore_signal(
            barrier, inc=1, device_id=dev(s, peer // cols_n, lax.rem(peer, cols_n)),
            device_id_type=MESH,
        )

    each(group - 1, greet)
    expected = group - 1 + jnp.int32(0)
    for dr, dc in SPREAD:
        expected = expected + jnp.where((s > 0) & inside(dr, dc), 1, 0)

        @pl.when((s < sections - 1) & inside(dr, dc))
        def _():
            pl.semaphore_signal(
                barrier, inc=1, device_id=dev(s + 1, r + dr, c + dc), device_id_type=MESH
            )

    pl.semaphore_wait(barrier, expected)

    halos = ((p2_ref, p2f), (x_ref, xf), (p1_ref, p1f))
    around = [(d, dr, dc) for d, (dr, dc) in enumerate(SPREAD) if (dr, dc) != (0, 0)]

    def halo_copy(m, which, d, dr, dc):
        src, dst = halos[which]
        return shift_copy(
            src, dst, m, dr, dc, halo_send.at[m, which, d], halo_recv.at[m, which, d], s
        )

    def out_grad_copy(m, d, dr, dc):
        return shift_copy(og_ref, gf, m, dr, dc, og_send.at[m, d], g_recv.at[m, d], s)

    def section_copy(m, d, dr, dc):
        return shift_copy(
            out_ref, gf, m, dr, dc, g_send.at[m, d], g_recv.at[m, d], s - 1
        )

    for m in range(micros):
        for d, dr, dc in around:

            @pl.when(inside(dr, dc) & (s == sections - 1))
            def _():
                out_grad_copy(m, d, dr, dc).start()

            @pl.when(inside(dr, dc))
            def _():
                for which in range(3):
                    halo_copy(m, which, d, dr, dc).start()

    for conv in range(2):
        for k in range(9):
            kt[conv, pl.ds(k * width, width), :] = jnp.transpose(k_ref[conv, 8 - k])

    for src, dst in halos:
        dst[:, pl.ds(2, rows), pl.ds(0, cols), :] = src[...]

    @pl.when(s == sections - 1)
    def _():
        gf[:, pl.ds(2, rows), pl.ds(0, cols), :] = og_ref[...]

    g0 = scale_ref[0:1, :].reshape(1, 1, width)
    g1 = scale_ref[1:2, :].reshape(1, 1, width)
    b0 = shift_ref[0:1, :].reshape(1, 1, width)
    b1 = shift_ref[1:2, :].reshape(1, 1, width)
    for m in range(micros):
        first_norm = g0 * p1_ref[m].astype(F32) + b0
        act[pl.ds(m * rows * cols, rows * cols), :] = (
            jnp.maximum(first_norm, 0.0).astype(BF16).reshape(rows * cols, width)
        )

    row_i = lax.broadcasted_iota(jnp.int32, (rows + 2, pitch, width), 0)
    col_i = lax.broadcasted_iota(jnp.int32, (rows + 2, pitch, width), 1)
    row_lo = jnp.where(r == 0, 1, 0)
    row_hi = jnp.where(r == rows_n - 1, rows, rows + 1)
    col_hi = jnp.where(c == cols_n - 1, cols, cols + half)
    col_lo = jnp.where(c == 0, pitch, cols + half)
    valid = (
        (row_i >= row_lo) & (row_i <= row_hi) & ((col_i < col_hi) | (col_i >= col_lo))
    )

    def wrapped(field):
        left = pltpu.roll(field, 1, 1)
        right = pltpu.roll(field, pitch - 1, 1)
        return left.astype(BF16), field.astype(BF16), right.astype(BF16)

    for m in range(micros):
        for d, dr, dc in around:

            @pl.when(inside(-dr, -dc))
            def _():
                for which in range(3):
                    halo_copy(m, which, d, dr, dc).wait_recv()

        second_norm = g1 * p2f[m].astype(F32) + b1
        c2[...] = jnp.where(second_norm + xf[m].astype(F32) > 0, g1, 0.0)
        first_norm = g0 * p1f[m, pl.ds(1, rows + 2)].astype(F32) + b0
        c1[...] = jnp.where((first_norm > 0) & valid, g0, 0.0)

        for d, (dr, dc) in enumerate(SPREAD):
            if (dr, dc) == (0, 0):

                @pl.when(s < sections - 1)
                def _():
                    section_copy(m, d, dr, dc).wait_recv()
            else:

                @pl.when(inside(-dr, -dc))
                def _():
                    section_copy(m, d, dr, dc).wait_recv()

        incoming = gf[m].astype(F32)
        second_grad = (incoming * c2[...]).astype(BF16).astype(F32)
        acc = None
        moved = wrapped(second_grad)
        base = m * rows * cols
        for i in range(3):
            for j in range(3):
                k = 3 * i + j
                part = moved[j][i : i + rows + 2]
                cols2[pl.ds(base, rows * cols), pl.ds(k * width, width)] = part[
                    1 : rows + 1, :cols
                ].reshape(rows * cols, width)
                term = jnp.dot(
                    part.reshape((rows + 2) * pitch, width),
                    kt[1, pl.ds(k * width, width), :],
                    preferred_element_type=F32,
                )
                acc = term if acc is None else acc + term
        first_grad = (acc.reshape(rows + 2, pitch, width) * c1[...]).astype(BF16).astype(F32)
        moved = wrapped(first_grad)
        for i in range(3):
            for j in range(3):
                k = 3 * i + j
                cols1[pl.ds(base, rows * cols), pl.ds(k * width, width)] = moved[j][
                    i : i + rows, :cols
                ].reshape(rows * cols, width)
        back = jnp.dot(
            cols1[pl.ds(base, rows * cols), :], kt[0], preferred_element_type=F32
        )
        tile = (pl.ds(2, rows), pl.ds(0, cols))
        masked = jnp.where(c2[tile] > 0, gf[(m, *tile)].astype(F32), 0.0)
        out_ref[m] = (masked + back.reshape(rows, cols, width)).astype(BF16)
        for d, (dr, dc) in enumerate(SPREAD):

            @pl.when((s > 0) & inside(dr, dc))
            def _():
                section_copy(m, d, dr, dc).start()

    if red.shape[0] > 18 * width:
        red[pl.ds(18 * width, red.shape[0] - 18 * width), :] = jnp.zeros(
            (red.shape[0] - 18 * width, width), BF16
        )
    pixels = micros * rows * cols
    contract = (((0,), (0,)), ((), ()))
    fields = (x_ref[...].reshape(pixels, width), act[...])
    for conv, grads in ((1, cols2), (0, cols1)):
        total = lax.dot_general(fields[conv], grads[...], contract, preferred_element_type=F32)
        for k in range(9):
            red[pl.ds((conv * 9 + 8 - k) * width, width), :] = (
                total[:, k * width : (k + 1) * width] * factor
            ).astype(BF16)

    def piece(index):
        return pl.ds(pl.multiple_of(index * chunk, 16), chunk)

    def peer_of(step):
        peer = lax.rem(me + step + 1, group)
        return peer, dev(s, peer // cols_n, lax.rem(peer, cols_n))

    def rs_copy(step):
        peer, where = peer_of(step)
        return pltpu.make_async_remote_copy(
            src_ref=red.at[piece(peer)], dst_ref=inbox.at[step],
            send_sem=rs_send.at[step], recv_sem=rs_recv.at[step],
            device_id=where, device_id_type=MESH,
        )

    def ag_copy(step):
        peer, where = peer_of(step)
        return pltpu.make_async_remote_copy(
            src_ref=final, dst_ref=gathered.at[step],
            send_sem=ag_send.at[step], recv_sem=ag_recv.at[step],
            device_id=where, device_id_type=MESH,
        )

    each(group - 1, lambda step: rs_copy(step).start())
    fg_ref[piece(me), :] = red[piece(me), :].astype(F32)

    def gather_in(step):
        rs_copy(step).wait_recv()
        fg_ref[piece(me), :] += inbox[step].astype(F32)

    each(group - 1, gather_in)
    final[...] = fg_ref[piece(me), :].astype(BF16)
    each(group - 1, lambda step: ag_copy(step).start())

    def spread_out(step):
        ag_copy(step).wait_recv()
        source = lax.rem(me + group - step - 1, group)
        fg_ref[piece(source), :] = gathered[step].astype(F32)

    each(group - 1, spread_out)

    each(group - 1, lambda step: rs_copy(step).wait_send())
    each(group - 1, lambda step: ag_copy(step).wait_send())
    for m in range(micros):
        for d, (dr, dc) in enumerate(SPREAD):
            if (dr, dc) != (0, 0):

                @pl.when(inside(dr, dc))
                def _():
                    for which in range(3):
                        halo_copy(m, which, d, dr, dc).wait_send()

                @pl.when(inside(dr, dc) & (s == sections - 1))
                def _():
                    out_grad_copy(m, d, dr, dc).wait_send()

            @pl.when((s > 0) & inside(dr, dc))
            def _():
                section_copy(m, d, dr, dc).wait_send()


def on_device(axes, sizes, section_input, first_pre, second_pre, out_grad, kernels, bn_scale, bn_shift):
    sections, rows_n, cols_n = sizes
    micros, rows, cols, width = out_grad.shape
    group = rows_n * cols_n
    tiles = 18 * width // 16
    chunk = 16 * (-(-tiles // group))
    pixels = micros * rows * cols
    factor = 1.0 / (pixels * group) ** 0.5
    dims = (axes, sections, rows_n, cols_n, factor)
    pitch = 2 * cols
    dma = pltpu.SemaphoreType.DMA
    vmem = pl.BlockSpec(memory_space=pltpu.VMEM)
    field = pltpu.VMEM((micros, rows + 4, pitch, width), BF16)
    peers = max(group - 1, 1)
    out, grads = pl.pallas_call(
        functools.partial(kernel, dims),
        out_shape=(
            jax.ShapeDtypeStruct(out_grad.shape, BF16),
            jax.ShapeDtypeStruct((group * chunk, width), F32),
        ),
        in_specs=[vmem] * 7,
        out_specs=(vmem, vmem),
        scratch_shapes=[
            field, field, field, field,
            pltpu.VMEM((2, 9 * width, width), BF16),
            pltpu.VMEM((rows + 2, pitch, width), F32),
            pltpu.VMEM((rows + 4, pitch, width), F32),
            pltpu.VMEM((pixels, 9 * width), BF16),
            pltpu.VMEM((pixels, 9 * width), BF16),
            pltpu.VMEM((pixels, width), BF16),
            pltpu.VMEM((group * chunk, width), BF16),
            pltpu.VMEM((peers, chunk, width), BF16),
            pltpu.VMEM((chunk, width), BF16),
            pltpu.VMEM((peers, chunk, width), BF16),
            dma((micros, 3, 9)), dma((micros, 3, 9)),
            dma((micros, 9)), dma((micros, 9)), dma((micros, 9)),
            dma((peers,)), dma((peers,)), dma((peers,)), dma((peers,)),
        ],
        compiler_params=pltpu.CompilerParams(
            collective_id=0, has_side_effects=True, vmem_limit_bytes=48 * 1024 * 1024
        ),
    )(
        section_input[0], first_pre[0], second_pre[0], out_grad,
        kernels[0].reshape(2, 9, width, width), bn_scale[0], bn_shift[0],
    )
    grads = grads[: 18 * width].reshape(1, 2, 3, 3, width, width)
    return out[None], grads


def solution(mesh):
    in_specs = (
        P("section", None, "row", "col", None),
        P("section", None, "row", "col", None),
        P("section", None, "row", "col", None),
        P(None, "row", "col", None),
        P("section", None, None, None, None, None),
        P("section", None, None),
        P("section", None, None),
    )
    out_specs = (P("section", None, "row", "col", None), P("section", None, None, None, None, None))
    sizes = tuple(mesh.shape[a] for a in ("section", "row", "col"))
    return jax.shard_map(
        functools.partial(on_device, tuple(mesh.axis_names), sizes),
        mesh=mesh, in_specs=in_specs, out_specs=out_specs, check_vma=False,
    )
```

time: 270 us -> 59.9 us (0.22)
  waiting for transfers between devices: 150 us -> 0 us
  starting transfers between devices: 87.4 us -> 0 us
  Pallas kernels: 0 us -> 51.4 us
  between operations: 15.6 us -> 0.66 us
  other arithmetic: 9.12 us -> 0 us
  local copies, waits for them, and re-layouts: 2.39 us -> 7.41 us
  matrix products: 3.61 us -> 0 us
    ppermute x48 -> x0, starting transfers between devices: 87.4 us -> none  [the longest x22 53.8 us: padded_2(): lax.ppermute(tail, axis, [(i, (i + 1) % count) for i in range(ends)])]
    ppermute x48 -> x0, waiting for transfers between devices: 86.3 us -> none  [the longest x22 80.9 us: padded_2(): lax.ppermute(head, axis, [((i + 1) % count, i) for i in range(ends)])]
    psum x1 -> x0, waiting for transfers between devices: 64.2 us -> none  [on_device(): summed = lax.psum(filter_acc, ('row', 'col'))]
    pallas_call x0 -> x1, Pallas kernels: none -> 51.4 us  [on_device(): pl.pallas_call(functools.partial(kernel, dims), out_shape=(jax.ShapeDtype...]
    unnamed x27 -> x16, local copies, waits for them, and re-layouts: 0.44 us -> 7.41 us
    conv_general_dilated x10 -> x0, matrix products: 2.87 us -> none  [correlate(): lax.conv_general_dilated(padded[None], kernel, (1, 1), 'VALID', dimension...]
    broadcast_in_dim x11 -> x0, other arithmetic: 2.74 us -> none  [the longest x1 2.42 us: on_device(): return (outputs[None], (summed * factor)[None])]
  transfers between devices with their start and end apart: 49 -> 0, of which waited for: 24 -> 0; matrix products, arithmetic and copies ran while one was open for 2% -> 0% of each run, Pallas kernels for 0% -> 0%
where the time goes in v1:
time: 59.9 us; the launch traced here: 59.5 us
  Pallas kernels  51.4 us (86%)
  local copies, waits for them, and re-layouts  7.41 us (12%)
  between operations  0.66 us (1%)
    pallas_call x1, Pallas kernels, on_device(): pl.pallas_call(functools.partial(kernel, dims), out_shape=(jax.ShapeDtype...  51.4 us
    unnamed x16, local copies, waits for them, and re-layouts  7.41 us

profile of v1, /device:TPU:0, one launch (start us, length us, event | category | flops | bytes accessed | tf_op | source)
XLA Modules:
  0.0 59.5 jit_solution(214726455438527749)
XLA Ops:
  0.6 0.0 copy-start
  0.6 1.1 %copy-done = bf16[1,2,3,3,128,128]{5,4,3,2,1,0:T(8,128)(2,1)S(1)} copy-done((bf16[1,2,3,3,128,128]{5,4,3,2,1,0:T(8,128)(2,1)S(1)}, bf16[1,2,3,3,128,128]{5,4,3,2,1,0:T(8,128)(2,1)}, u32[]{:S(2)}) %copy-start) | copy-done | bytes 589848
  1.7 0.0 copy-start.1
  1.7 0.8 %copy-done.1 = bf16[1,2,8,16,128]{4,3,2,1,0:T(8,128)(2,1)S(1)} copy-done((bf16[1,2,8,16,128]{4,3,2,1,0:T(8,128)(2,1)S(1)}, bf16[1,2,8,16,128]{4,3,2,1,0:T(8,128)(2,1)}, u32[]{:S(2)}) %copy-start.1) | copy-done | bytes 65560
  2.5 0.0 copy-start.2
  2.5 0.8 %copy-done.2 = bf16[1,2,8,16,128]{4,3,2,1,0:T(8,128)(2,1)S(1)} copy-done((bf16[1,2,8,16,128]{4,3,2,1,0:T(8,128)(2,1)S(1)}, bf16[1,2,8,16,128]{4,3,2,1,0:T(8,128)(2,1)}, u32[]{:S(2)}) %copy-start.2) | copy-done | bytes 65560
  3.4 0.0 copy-start.3
  3.4 0.8 %copy-done.3 = bf16[1,2,8,16,128]{4,3,2,1,0:T(8,128)(2,1)S(1)} copy-done((bf16[1,2,8,16,128]{4,3,2,1,0:T(8,128)(2,1)S(1)}, bf16[1,2,8,16,128]{4,3,2,1,0:T(8,128)(2,1)}, u32[]{:S(2)}) %copy-start.3) | copy-done | bytes 65560
  4.2 0.0 copy-start.4
  4.2 0.8 %copy-done.4 = bf16[2,8,16,128]{3,2,1,0:T(8,128)(2,1)S(1)} copy-done((bf16[2,8,16,128]{3,2,1,0:T(8,128)(2,1)S(1)}, bf16[2,8,16,128]{3,2,1,0:T(8,128)(2,1)}, u32[]{:S(2)}) %copy-start.4) | copy-done | bytes 65560
  5.1 0.0 copy-start.5
  5.1 0.7 %copy-done.5 = f32[1,2,128]{2,1,0:T(2,128)S(1)} copy-done((f32[1,2,128]{2,1,0:T(2,128)S(1)}, f32[1,2,128]{2,1,0:T(2,128)}, u32[]{:S(2)}) %copy-start.5) | copy-done | bytes 1048
  5.7 0.0 copy-start.6
  5.7 0.7 %copy-done.6 = f32[1,2,128]{2,1,0:T(2,128)S(1)} copy-done((f32[1,2,128]{2,1,0:T(2,128)S(1)}, f32[1,2,128]{2,1,0:T(2,128)}, u32[]{:S(2)}) %copy-start.6) | copy-done | bytes 1048
  6.4 51.4 %shard_map.86 = (bf16[2,8,16,128]{3,2,1,0:T(8,128)(2,1)S(1)}, f32[2304,128]{1,0:T(8,128)S(1)}) custom-call(bf16[2,8,16,128]{3,2,1,0:T(8,128)(2,1)S(1)} %bitcast.11, bf16[2,8,16,128]{3,2,1,0:T(8,128)(2,1)S(1)} %bitcast.12, bf16[2,8,16,128]{3,2,1,0:T(8,128)(2,1)S(1)} %bitcast.13, bf16[2,8,16,128]{3,2,1,0:T(8,128)(2,1)S(1)} %copy-done.4, ...), custom_call_target="tpu_custom_call" | custom-call | tf_op jit(solution)/shard_map/pallas_call | solution.py:314
  57.9 0.6 %copy.11 = bf16[1,2,8,16,128]{4,3,2,1,0:T(8,128)(2,1)} copy(bf16[1,2,8,16,128]{4,3,2,1,0:T(8,128)(2,1)S(1)} %bitcast.10) | data formatting | bytes 131072
  58.5 1.0 %copy.12 = f32[1,2,3,3,128,128]{5,4,3,2,1,0:T(8,128)} copy(f32[1,2,3,3,128,128]{5,4,3,2,1,0:T(8,128)S(1)} %bitcast.8) | data formatting | bytes 2359296
Async XLA Ops:
  0.6 1.1 %copy-start = (bf16[1,2,3,3,128,128]{5,4,3,2,1,0:T(8,128)(2,1)S(1)}, bf16[1,2,3,3,128,128]{5,4,3,2,1,0:T(8,128)(2,1)}, u32[]{:S(2)}) copy-start(bf16[1,2,3,3,128,128]{5,4,3,2,1,0:T(8,128)(2,1)} %param.11) | copy-start | bytes 1769476
  1.7 0.8 %copy-start.1 = (bf16[1,2,8,16,128]{4,3,2,1,0:T(8,128)(2,1)S(1)}, bf16[1,2,8,16,128]{4,3,2,1,0:T(8,128)(2,1)}, u32[]{:S(2)}) copy-start(bf16[1,2,8,16,128]{4,3,2,1,0:T(8,128)(2,1)} %param.7) | copy-start | bytes 196612
  2.5 0.8 %copy-start.2 = (bf16[1,2,8,16,128]{4,3,2,1,0:T(8,128)(2,1)S(1)}, bf16[1,2,8,16,128]{4,3,2,1,0:T(8,128)(2,1)}, u32[]{:S(2)}) copy-start(bf16[1,2,8,16,128]{4,3,2,1,0:T(8,128)(2,1)} %param.8) | copy-start | bytes 196612
  3.4 0.8 %copy-start.3 = (bf16[1,2,8,16,128]{4,3,2,1,0:T(8,128)(2,1)S(1)}, bf16[1,2,8,16,128]{4,3,2,1,0:T(8,128)(2,1)}, u32[]{:S(2)}) copy-start(bf16[1,2,8,16,128]{4,3,2,1,0:T(8,128)(2,1)} %param.9) | copy-start | bytes 196612
  4.2 0.8 %copy-start.4 = (bf16[2,8,16,128]{3,2,1,0:T(8,128)(2,1)S(1)}, bf16[2,8,16,128]{3,2,1,0:T(8,128)(2,1)}, u32[]{:S(2)}) copy-start(bf16[2,8,16,128]{3,2,1,0:T(8,128)(2,1)} %og_ref.1) | copy-start | bytes 196612
  5.1 0.7 %copy-start.5 = (f32[1,2,128]{2,1,0:T(2,128)S(1)}, f32[1,2,128]{2,1,0:T(2,128)}, u32[]{:S(2)}) copy-start(f32[1,2,128]{2,1,0:T(2,128)} %param.12) | copy-start | bytes 3076
  5.7 0.7 %copy-start.6 = (f32[1,2,128]{2,1,0:T(2,128)S(1)}, f32[1,2,128]{2,1,0:T(2,128)}, u32[]{:S(2)}) copy-start(f32[1,2,128]{2,1,0:T(2,128)} %param.13) | copy-start | bytes 3076

commit v2 on v1

--- a/solution.py
+++ b/solution.py
@@ -27,12 +27,13 @@
 
 
 def kernel(
-    dims, x_ref, p1_ref, p2_ref, og_ref, k_ref, scale_ref, shift_ref,
+    dims, x_ref, p1_ref, p2_ref, og_ref, k_hbm, scale_hbm, shift_hbm,
     out_ref, fg_ref,
-    xf, p1f, p2f, gf, kt, c1, c2, cols1, cols2, act, red, inbox, final, gathered,
-    halo_send, halo_recv, og_send, g_send, g_recv, rs_send, rs_recv, ag_send, ag_recv,
+    xf, p1f, p2f, gf, k_ref, scale_ref, shift_ref, kt, c1, c2, cols1, cols2, act,
+    union_x, union_g, spare_x, spare_g, crossed, red, inbox, final, gathered,
+    local, pair_send, pair_recv, halo_send, halo_recv, og_send, g_send, g_recv, rs_send, rs_recv, ag_send, ag_recv,
 ):
-    axes, sections, rows_n, cols_n, factor = dims
+    axes, sections, rows_n, cols_n, factor, paired = dims
     micros, rows, cols, width = x_ref.shape
     pitch = 2 * cols
     half = cols // 2
@@ -63,14 +64,40 @@
     def shift_copy(src, dst, m, dr, dc, send, recv, sec):
         a, b = src_part(dr, dc)
         p, q = dst_part(dr, dc)
+        if src is dst:
+            a = pl.ds(a.start + 2, a.size)
         return pltpu.make_async_remote_copy(
             src_ref=src.at[m, a, b], dst_ref=dst.at[m, p, q],
             send_sem=send, recv_sem=recv,
             device_id=dev(sec, r + dr, c + dc), device_id_type=MESH,
         )
 
+    def centre(ref):
+        return ref.at[:, pl.ds(2, rows), pl.ds(0, cols)]
+
+    loads = [
+        pltpu.make_async_copy(src, dst, local.at[i])
+        for i, (src, dst) in enumerate(
+            (
+                (p2_ref, centre(p2f)), (x_ref, centre(xf)), (p1_ref, centre(p1f)),
+                (scale_hbm, scale_ref), (shift_hbm, shift_ref), (k_hbm, k_ref),
+            )
+        )
+    ]
+    og_load = pltpu.make_async_copy(og_ref, centre(gf), local.at[6])
+
+    @pl.when(s == sections - 1)
+    def _():
+        og_load.start()
+
+    for load in loads:
+        load.start()
+
     for ref in (xf, p1f, p2f, gf):
-        ref[...] = jnp.zeros(ref.shape, ref.dtype)
+        for m in range(micros):
+            ref[m, 0:2] = jnp.zeros((2, pitch, width), BF16)
+            ref[m, rows + 2 : rows + 4] = jnp.zeros((2, pitch, width), BF16)
+            ref[m, 2 : rows + 2, cols:pitch] = jnp.zeros((rows, cols, width), BF16)
 
     barrier = pltpu.get_barrier_semaphore()
 
@@ -92,9 +119,16 @@
                 barrier, inc=1, device_id=dev(s + 1, r + dr, c + dc), device_id_type=MESH
             )
 
+    for load in loads[:3]:
+        load.wait()
+
+    @pl.when(s == sections - 1)
+    def _():
+        og_load.wait()
+
     pl.semaphore_wait(barrier, expected)
 
-    halos = ((p2_ref, p2f), (x_ref, xf), (p1_ref, p1f))
+    halos = ((p2f, p2f), (xf, xf), (p1f, p1f))
     around = [(d, dr, dc) for d, (dr, dc) in enumerate(SPREAD) if (dr, dc) != (0, 0)]
 
     def halo_copy(m, which, d, dr, dc):
@@ -104,7 +138,7 @@
         )
 
     def out_grad_copy(m, d, dr, dc):
-        return shift_copy(og_ref, gf, m, dr, dc, og_send.at[m, d], g_recv.at[m, d], s)
+        return shift_copy(gf, gf, m, dr, dc, og_send.at[m, d], g_recv.at[m, d], s)
 
     def section_copy(m, d, dr, dc):
         return shift_copy(
@@ -123,26 +157,46 @@
                 for which in range(3):
                     halo_copy(m, which, d, dr, dc).start()
 
+    for load in loads[3:]:
+        load.wait()
     for conv in range(2):
         for k in range(9):
             kt[conv, pl.ds(k * width, width), :] = jnp.transpose(k_ref[conv, 8 - k])
-
-    for src, dst in halos:
-        dst[:, pl.ds(2, rows), pl.ds(0, cols), :] = src[...]
-
-    @pl.when(s == sections - 1)
-    def _():
-        gf[:, pl.ds(2, rows), pl.ds(0, cols), :] = og_ref[...]
 
     g0 = scale_ref[0:1, :].reshape(1, 1, width)
     g1 = scale_ref[1:2, :].reshape(1, 1, width)
     b0 = shift_ref[0:1, :].reshape(1, 1, width)
     b1 = shift_ref[1:2, :].reshape(1, 1, width)
+    own = pl.ds(pl.multiple_of(c * cols, cols), cols)
+
+    def pair_copy(m, which, src, dst):
+        return pltpu.make_async_remote_copy(
+            src_ref=src.at[m], dst_ref=dst.at[m, :, own],
+            send_sem=pair_send.at[m, which], recv_sem=pair_recv.at[m, which],
+            device_id=dev(s, r, 1 - c), device_id_type=MESH,
+        )
+
+    def pair_arrival(m, which, src, dst):
+        other = pl.ds(pl.multiple_of((1 - c) * cols, cols), cols)
+        return pltpu.make_async_remote_copy(
+            src_ref=src.at[m], dst_ref=dst.at[m, :, other],
+            send_sem=pair_send.at[m, which], recv_sem=pair_recv.at[m, which],
+            device_id=dev(s, r, 1 - c), device_id_type=MESH,
+        )
+
+    pairs = ((spare_x, union_x), (spare_g, union_g))
     for m in range(micros):
-        first_norm = g0 * p1_ref[m].astype(F32) + b0
-        act[pl.ds(m * rows * cols, rows * cols), :] = (
-            jnp.maximum(first_norm, 0.0).astype(BF16).reshape(rows * cols, width)
-        )
+        first_norm = g0 * p1f[m, 2 : rows + 2, :cols].astype(F32) + b0
+        active = jnp.maximum(first_norm, 0.0)
+        if paired:
+            inputs = xf[m, 2 : rows + 2, :cols].astype(F32)
+            union_x[m, :, own] = jnp.where(c == 0, inputs, active).astype(BF16)
+            spare_x[m] = jnp.where(c == 0, active, inputs).astype(BF16)
+            pair_copy(m, 0, *pairs[0]).start()
+        else:
+            act[pl.ds(m * rows * cols, rows * cols), :] = active.astype(BF16).reshape(
+                rows * cols, width
+            )
 
     row_i = lax.broadcasted_iota(jnp.int32, (rows + 2, pitch, width), 0)
     col_i = lax.broadcasted_iota(jnp.int32, (rows + 2, pitch, width), 1)
@@ -193,9 +247,10 @@
             for j in range(3):
                 k = 3 * i + j
                 part = moved[j][i : i + rows + 2]
-                cols2[pl.ds(base, rows * cols), pl.ds(k * width, width)] = part[
-                    1 : rows + 1, :cols
-                ].reshape(rows * cols, width)
+                if not paired:
+                    cols2[pl.ds(base, rows * cols), pl.ds(k * width, width)] = part[
+                        1 : rows + 1, :cols
+                    ].reshape(rows * cols, width)
                 term = jnp.dot(
                     part.reshape((rows + 2) * pitch, width),
                     kt[1, pl.ds(k * width, width), :],
@@ -203,6 +258,12 @@
                 )
                 acc = term if acc is None else acc + term
         first_grad = (acc.reshape(rows + 2, pitch, width) * c1[...]).astype(BF16).astype(F32)
+        if paired:
+            second_own = second_grad[1 : rows + 3, :cols]
+            first_own = first_grad[:, :cols]
+            union_g[m, :, own] = jnp.where(c == 0, first_own, second_own).astype(BF16)
+            spare_g[m] = jnp.where(c == 0, second_own, first_own).astype(BF16)
+            pair_copy(m, 1, *pairs[1]).start()
         moved = wrapped(first_grad)
         for i in range(3):
             for j in range(3):
@@ -222,63 +283,147 @@
             def _():
                 section_copy(m, d, dr, dc).start()
 
-    if red.shape[0] > 18 * width:
-        red[pl.ds(18 * width, red.shape[0] - 18 * width), :] = jnp.zeros(
-            (red.shape[0] - 18 * width, width), BF16
-        )
-    pixels = micros * rows * cols
-    contract = (((0,), (0,)), ((), ()))
-    fields = (x_ref[...].reshape(pixels, width), act[...])
-    for conv, grads in ((1, cols2), (0, cols1)):
-        total = lax.dot_general(fields[conv], grads[...], contract, preferred_element_type=F32)
+    if paired:
+        area = rows * pitch
+        edge = lax.broadcasted_iota(jnp.int32, (rows + 2, pitch, width), 1)
+        for m in range(micros):
+            for which in range(2):
+                pair_arrival(m, which, *pairs[which]).wait_recv()
+            field = union_g[m].astype(F32)
+            moved = (
+                jnp.where(edge > 0, pltpu.roll(field, 1, 1), 0.0).astype(BF16),
+                union_g[m],
+                jnp.where(edge < pitch - 1, pltpu.roll(field, pitch - 1, 1), 0.0).astype(BF16),
+            )
+            for i in range(3):
+                for j in range(3):
+                    cols2[
+                        pl.ds(m * area, area), pl.ds((3 * i + j) * width, width)
+                    ] = moved[j][i : i + rows].reshape(area, width)
+        total = lax.dot_general(
+            union_x[...].reshape(micros * area, width), cols2[...],
+            (((0,), (0,)), ((), ())), preferred_element_type=F32,
+        )
         for k in range(9):
-            red[pl.ds((conv * 9 + 8 - k) * width, width), :] = (
+            red[pl.ds((8 - k) * width, width), :] = (
                 total[:, k * width : (k + 1) * width] * factor
             ).astype(BF16)
 
-    def piece(index):
-        return pl.ds(pl.multiple_of(index * chunk, 16), chunk)
-
-    def peer_of(step):
-        peer = lax.rem(me + step + 1, group)
-        return peer, dev(s, peer // cols_n, lax.rem(peer, cols_n))
-
-    def rs_copy(step):
-        peer, where = peer_of(step)
-        return pltpu.make_async_remote_copy(
-            src_ref=red.at[piece(peer)], dst_ref=inbox.at[step],
-            send_sem=rs_send.at[step], recv_sem=rs_recv.at[step],
-            device_id=where, device_id_type=MESH,
-        )
-
-    def ag_copy(step):
-        peer, where = peer_of(step)
-        return pltpu.make_async_remote_copy(
-            src_ref=final, dst_ref=gathered.at[step],
-            send_sem=ag_send.at[step], recv_sem=ag_recv.at[step],
-            device_id=where, device_id_type=MESH,
-        )
-
-    each(group - 1, lambda step: rs_copy(step).start())
-    fg_ref[piece(me), :] = red[piece(me), :].astype(F32)
-
-    def gather_in(step):
-        rs_copy(step).wait_recv()
-        fg_ref[piece(me), :] += inbox[step].astype(F32)
-
-    each(group - 1, gather_in)
-    final[...] = fg_ref[piece(me), :].astype(BF16)
-    each(group - 1, lambda step: ag_copy(step).start())
-
-    def spread_out(step):
-        ag_copy(step).wait_recv()
-        source = lax.rem(me + group - step - 1, group)
-        fg_ref[piece(source), :] = gathered[step].astype(F32)
-
-    each(group - 1, spread_out)
-
-    each(group - 1, lambda step: rs_copy(step).wait_send())
-    each(group - 1, lambda step: ag_copy(step).wait_send())
+        def row_piece(index):
+            return pl.ds(pl.multiple_of(index * chunk, 16), chunk)
+
+        def out_piece(conv, index):
+            return pl.ds(pl.multiple_of((conv * rows_n + index) * chunk, 16), chunk)
+
+        def row_copy(step, src, dst, send, recv):
+            peer = lax.rem(r + step + 1, rows_n)
+            return pltpu.make_async_remote_copy(
+                src_ref=red.at[row_piece(peer)] if src is red else src, dst_ref=dst.at[step],
+                send_sem=send.at[step], recv_sem=recv.at[step],
+                device_id=dev(s, peer, c), device_id_type=MESH,
+            )
+
+        def cross_copy(step):
+            return pltpu.make_async_remote_copy(
+                src_ref=gathered.at[step] if step < rows_n - 1 else final,
+                dst_ref=crossed.at[step],
+                send_sem=rs_send.at[rows_n + step], recv_sem=rs_recv.at[rows_n + step],
+                device_id=dev(s, r, 1 - c), device_id_type=MESH,
+            )
+
+        def sum_copy(step):
+            return row_copy(step, red, inbox, rs_send, rs_recv)
+
+        def spread_copy(step):
+            return row_copy(step, final, gathered, ag_send, ag_recv)
+
+        for step in range(rows_n - 1):
+            sum_copy(step).start()
+        summed = red[row_piece(r), :].astype(F32)
+        for step in range(rows_n - 1):
+            sum_copy(step).wait_recv()
+            summed = summed + inbox[step].astype(F32)
+        final[...] = summed.astype(BF16)
+        for step in range(rows_n - 1):
+            spread_copy(step).start()
+        cross_copy(rows_n - 1).start()
+        fg_ref[out_piece(c, r), :] = final[...].astype(F32)
+        for step in range(rows_n - 1):
+            spread_copy(step).wait_recv()
+            cross_copy(step).start()
+            source = lax.rem(r + rows_n - step - 1, rows_n)
+            fg_ref[out_piece(c, source), :] = gathered[step].astype(F32)
+        for step in [rows_n - 1, *range(rows_n - 1)]:
+            cross_copy(step).wait_recv()
+            source = lax.rem(r + 2 * rows_n - step - 1, rows_n)
+            fg_ref[out_piece(1 - c, source), :] = crossed[step].astype(F32)
+        for step in range(rows_n - 1):
+            sum_copy(step).wait_send()
+            spread_copy(step).wait_send()
+        for step in range(rows_n):
+            cross_copy(step).wait_send()
+        for m in range(micros):
+            for which in range(2):
+                pair_copy(m, which, *pairs[which]).wait_send()
+    else:
+        if red.shape[0] > 18 * width:
+            red[pl.ds(18 * width, red.shape[0] - 18 * width), :] = jnp.zeros(
+                (red.shape[0] - 18 * width, width), BF16
+            )
+        pixels = micros * rows * cols
+        contract = (((0,), (0,)), ((), ()))
+        inputs = xf[:, 2 : rows + 2, :cols].reshape(pixels, width)
+        fields = (inputs, act[...])
+        for conv, grads in ((1, cols2), (0, cols1)):
+            total = lax.dot_general(fields[conv], grads[...], contract, preferred_element_type=F32)
+            for k in range(9):
+                red[pl.ds((conv * 9 + 8 - k) * width, width), :] = (
+                    total[:, k * width : (k + 1) * width] * factor
+                ).astype(BF16)
+
+        def piece(index):
+            return pl.ds(pl.multiple_of(index * chunk, 16), chunk)
+
+        def peer_of(step):
+            peer = lax.rem(me + step + 1, group)
+            return peer, dev(s, peer // cols_n, lax.rem(peer, cols_n))
+
+        def rs_copy(step):
+            peer, where = peer_of(step)
+            return pltpu.make_async_remote_copy(
+                src_ref=red.at[piece(peer)], dst_ref=inbox.at[step],
+                send_sem=rs_send.at[step], recv_sem=rs_recv.at[step],
+                device_id=where, device_id_type=MESH,
+            )
+
+        def ag_copy(step):
+            peer, where = peer_of(step)
+            return pltpu.make_async_remote_copy(
+                src_ref=final, dst_ref=gathered.at[step],
+                send_sem=ag_send.at[step], recv_sem=ag_recv.at[step],
+                device_id=where, device_id_type=MESH,
+            )
+
+        each(group - 1, lambda step: rs_copy(step).start())
+        fg_ref[piece(me), :] = red[piece(me), :].astype(F32)
+
+        def gather_in(step):
+            rs_copy(step).wait_recv()
+            fg_ref[piece(me), :] += inbox[step].astype(F32)
+
+        each(group - 1, gather_in)
+        final[...] = fg_ref[piece(me), :].astype(BF16)
+        each(group - 1, lambda step: ag_copy(step).start())
+
+        def spread_out(step):
+            ag_copy(step).wait_recv()
+            source = lax.rem(me + group - step - 1, group)
+            fg_ref[piece(source), :] = gathered[step].astype(F32)
+
+        each(group - 1, spread_out)
+
+        each(group - 1, lambda step: rs_copy(step).wait_send())
+        each(group - 1, lambda step: ag_copy(step).wait_send())
     for m in range(micros):
         for d, (dr, dc) in enumerate(SPREAD):
             if (dr, dc) != (0, 0):
@@ -305,38 +450,50 @@
     chunk = 16 * (-(-tiles // group))
     pixels = micros * rows * cols
     factor = 1.0 / (pixels * group) ** 0.5
-    dims = (axes, sections, rows_n, cols_n, factor)
+    paired = cols_n == 2 and tiles % group == 0
+    dims = (axes, sections, rows_n, cols_n, factor, paired)
     pitch = 2 * cols
     dma = pltpu.SemaphoreType.DMA
     vmem = pl.BlockSpec(memory_space=pltpu.VMEM)
     field = pltpu.VMEM((micros, rows + 4, pitch, width), BF16)
     peers = max(group - 1, 1)
+    wide = micros * rows * pitch if paired else pixels
+    hbm = pl.BlockSpec(memory_space=pltpu.HBM)
     out, grads = pl.pallas_call(
         functools.partial(kernel, dims),
         out_shape=(
             jax.ShapeDtypeStruct(out_grad.shape, BF16),
             jax.ShapeDtypeStruct((group * chunk, width), F32),
         ),
-        in_specs=[vmem] * 7,
+        in_specs=[hbm] * 7,
         out_specs=(vmem, vmem),
         scratch_shapes=[
             field, field, field, field,
+            pltpu.VMEM((2, 9, width, width), BF16),
+            pltpu.VMEM((2, width), F32),
+            pltpu.VMEM((2, width), F32),
             pltpu.VMEM((2, 9 * width, width), BF16),
             pltpu.VMEM((rows + 2, pitch, width), F32),
             pltpu.VMEM((rows + 4, pitch, width), F32),
             pltpu.VMEM((pixels, 9 * width), BF16),
-            pltpu.VMEM((pixels, 9 * width), BF16),
+            pltpu.VMEM((wide, 9 * width), BF16),
             pltpu.VMEM((pixels, width), BF16),
+            pltpu.VMEM((micros, rows, pitch, width), BF16),
+            pltpu.VMEM((micros, rows + 2, pitch, width), BF16),
+            pltpu.VMEM((micros, rows, cols, width), BF16),
+            pltpu.VMEM((micros, rows + 2, cols, width), BF16),
+            pltpu.VMEM((rows_n, chunk, width), BF16),
             pltpu.VMEM((group * chunk, width), BF16),
             pltpu.VMEM((peers, chunk, width), BF16),
             pltpu.VMEM((chunk, width), BF16),
             pltpu.VMEM((peers, chunk, width), BF16),
+            dma((7,)), dma((micros, 2)), dma((micros, 2)),
             dma((micros, 3, 9)), dma((micros, 3, 9)),
             dma((micros, 9)), dma((micros, 9)), dma((micros, 9)),
-            dma((peers,)), dma((peers,)), dma((peers,)), dma((peers,)),
+            dma((group + rows_n,)), dma((group + rows_n,)), dma((peers,)), dma((peers,)),
         ],
         compiler_params=pltpu.CompilerParams(
-            collective_id=0, has_side_effects=True, vmem_limit_bytes=48 * 1024 * 1024
+            collective_id=0, has_side_effects=True, vmem_limit_bytes=40 * 1024 * 1024
         ),
     )(
         section_input[0], first_pre[0], second_pre[0], out_grad,

time: 59.9 us -> 55.8 us (0.932)
  Pallas kernels: 51.4 us -> 47.3 us
    pallas_call x1, Pallas kernels: 51.4 us -> 47.3 us  [on_device(): pl.pallas_call(functools.partial(kernel, dims), out_shape=(jax.ShapeDtype...]
where the time goes in v2:
time: 55.8 us; the launch traced here: 55.4 us
  Pallas kernels  47.3 us (85%)
  local copies, waits for them, and re-layouts  7.41 us (13%)
  between operations  0.66 us (1%)
    pallas_call x1, Pallas kernels, on_device(): pl.pallas_call(functools.partial(kernel, dims), out_shape=(jax.ShapeDtype...  47.3 us
    unnamed x16, local copies, waits for them, and re-layouts  7.41 us

profile of v2, /device:TPU:0, one launch (start us, length us, event | category | flops | bytes accessed | tf_op | source)
XLA Modules:
  0.0 55.4 jit_solution(9220969543132476074)
XLA Ops:
  0.6 0.0 copy-start
  0.6 1.1 %copy-done = bf16[1,2,3,3,128,128]{5,4,3,2,1,0:T(8,128)(2,1)S(1)} copy-done((bf16[1,2,3,3,128,128]{5,4,3,2,1,0:T(8,128)(2,1)S(1)}, bf16[1,2,3,3,128,128]{5,4,3,2,1,0:T(8,128)(2,1)}, u32[]{:S(2)}) %copy-start) | copy-done | bytes 589848
  1.7 0.0 copy-start.1
  1.7 0.8 %copy-done.1 = bf16[1,2,8,16,128]{4,3,2,1,0:T(8,128)(2,1)S(1)} copy-done((bf16[1,2,8,16,128]{4,3,2,1,0:T(8,128)(2,1)S(1)}, bf16[1,2,8,16,128]{4,3,2,1,0:T(8,128)(2,1)}, u32[]{:S(2)}) %copy-start.1) | copy-done | bytes 65560
  2.5 0.0 copy-start.2
  2.5 0.8 %copy-done.2 = bf16[1,2,8,16,128]{4,3,2,1,0:T(8,128)(2,1)S(1)} copy-done((bf16[1,2,8,16,128]{4,3,2,1,0:T(8,128)(2,1)S(1)}, bf16[1,2,8,16,128]{4,3,2,1,0:T(8,128)(2,1)}, u32[]{:S(2)}) %copy-start.2) | copy-done | bytes 65560
  3.4 0.0 copy-start.3
  3.4 0.8 %copy-done.3 = bf16[1,2,8,16,128]{4,3,2,1,0:T(8,128)(2,1)S(1)} copy-done((bf16[1,2,8,16,128]{4,3,2,1,0:T(8,128)(2,1)S(1)}, bf16[1,2,8,16,128]{4,3,2,1,0:T(8,128)(2,1)}, u32[]{:S(2)}) %copy-start.3) | copy-done | bytes 65560
  4.2 0.0 copy-start.4
  4.2 0.8 %copy-done.4 = bf16[2,8,16,128]{3,2,1,0:T(8,128)(2,1)S(1)} copy-done((bf16[2,8,16,128]{3,2,1,0:T(8,128)(2,1)S(1)}, bf16[2,8,16,128]{3,2,1,0:T(8,128)(2,1)}, u32[]{:S(2)}) %copy-start.4) | copy-done | bytes 65560
  5.1 0.0 copy-start.5
  5.1 0.7 %copy-done.5 = f32[1,2,128]{2,1,0:T(2,128)S(1)} copy-done((f32[1,2,128]{2,1,0:T(2,128)S(1)}, f32[1,2,128]{2,1,0:T(2,128)}, u32[]{:S(2)}) %copy-start.5) | copy-done | bytes 1048
  5.7 0.0 copy-start.6
  5.7 0.7 %copy-done.6 = f32[1,2,128]{2,1,0:T(2,128)S(1)} copy-done((f32[1,2,128]{2,1,0:T(2,128)S(1)}, f32[1,2,128]{2,1,0:T(2,128)}, u32[]{:S(2)}) %copy-start.6) | copy-done | bytes 1048
  6.4 47.3 %shard_map.86 = (bf16[2,8,16,128]{3,2,1,0:T(8,128)(2,1)S(1)}, f32[2304,128]{1,0:T(8,128)S(1)}) custom-call(bf16[2,8,16,128]{3,2,1,0:T(8,128)(2,1)S(1)} %bitcast.11, bf16[2,8,16,128]{3,2,1,0:T(8,128)(2,1)S(1)} %bitcast.12, bf16[2,8,16,128]{3,2,1,0:T(8,128)(2,1)S(1)} %bitcast.13, bf16[2,8,16,128]{3,2,1,0:T(8,128)(2,1)S(1)} %copy-done.4, ...), custom_call_target="tpu_custom_call" | custom-call | tf_op jit(solution)/shard_map/pallas_call | solution.py:462
  53.7 0.6 %copy.11 = bf16[1,2,8,16,128]{4,3,2,1,0:T(8,128)(2,1)} copy(bf16[1,2,8,16,128]{4,3,2,1,0:T(8,128)(2,1)S(1)} %bitcast.10) | data formatting | bytes 131072
  54.4 1.0 %copy.12 = f32[1,2,3,3,128,128]{5,4,3,2,1,0:T(8,128)} copy(f32[1,2,3,3,128,128]{5,4,3,2,1,0:T(8,128)S(1)} %bitcast.8) | data formatting | bytes 2359296
Async XLA Ops:
  0.6 1.1 %copy-start = (bf16[1,2,3,3,128,128]{5,4,3,2,1,0:T(8,128)(2,1)S(1)}, bf16[1,2,3,3,128,128]{5,4,3,2,1,0:T(8,128)(2,1)}, u32[]{:S(2)}) copy-start(bf16[1,2,3,3,128,128]{5,4,3,2,1,0:T(8,128)(2,1)} %param.11) | copy-start | bytes 1769476
  1.7 0.8 %copy-start.1 = (bf16[1,2,8,16,128]{4,3,2,1,0:T(8,128)(2,1)S(1)}, bf16[1,2,8,16,128]{4,3,2,1,0:T(8,128)(2,1)}, u32[]{:S(2)}) copy-start(bf16[1,2,8,16,128]{4,3,2,1,0:T(8,128)(2,1)} %param.7) | copy-start | bytes 196612
  2.5 0.8 %copy-start.2 = (bf16[1,2,8,16,128]{4,3,2,1,0:T(8,128)(2,1)S(1)}, bf16[1,2,8,16,128]{4,3,2,1,0:T(8,128)(2,1)}, u32[]{:S(2)}) copy-start(bf16[1,2,8,16,128]{4,3,2,1,0:T(8,128)(2,1)} %param.8) | copy-start | bytes 196612
  3.4 0.8 %copy-start.3 = (bf16[1,2,8,16,128]{4,3,2,1,0:T(8,128)(2,1)S(1)}, bf16[1,2,8,16,128]{4,3,2,1,0:T(8,128)(2,1)}, u32[]{:S(2)}) copy-start(bf16[1,2,8,16,128]{4,3,2,1,0:T(8,128)(2,1)} %param.9) | copy-start | bytes 196612
  4.2 0.8 %copy-start.4 = (bf16[2,8,16,128]{3,2,1,0:T(8,128)(2,1)S(1)}, bf16[2,8,16,128]{3,2,1,0:T(8,128)(2,1)}, u32[]{:S(2)}) copy-start(bf16[2,8,16,128]{3,2,1,0:T(8,128)(2,1)} %og_ref.1) | copy-start | bytes 196612
  5.1 0.7 %copy-start.5 = (f32[1,2,128]{2,1,0:T(2,128)S(1)}, f32[1,2,128]{2,1,0:T(2,128)}, u32[]{:S(2)}) copy-start(f32[1,2,128]{2,1,0:T(2,128)} %param.12) | copy-start | bytes 3076
  5.7 0.7 %copy-start.6 = (f32[1,2,128]{2,1,0:T(2,128)S(1)}, f32[1,2,128]{2,1,0:T(2,128)}, u32[]{:S(2)}) copy-start(f32[1,2,128]{2,1,0:T(2,128)} %param.13) | copy-start | bytes 3076

commit v3 on v2

--- a/solution.py
+++ b/solution.py
@@ -28,10 +28,10 @@
 
 def kernel(
     dims, x_ref, p1_ref, p2_ref, og_ref, k_hbm, scale_hbm, shift_hbm,
-    out_ref, fg_ref,
-    xf, p1f, p2f, gf, k_ref, scale_ref, shift_ref, kt, c1, c2, cols1, cols2, act,
+    out_hbm, fg_hbm,
+    out_ref, fg_ref, xf, p1f, p2f, gf, k_ref, scale_ref, shift_ref, kt, c1, c2, cols1, cols2, act,
     union_x, union_g, spare_x, spare_g, crossed, red, inbox, final, gathered,
-    local, pair_send, pair_recv, halo_send, halo_recv, og_send, g_send, g_recv, rs_send, rs_recv, ag_send, ag_recv,
+    stores, local, pair_send, pair_recv, halo_send, halo_recv, og_send, g_send, g_recv, rs_send, rs_recv, ag_send, ag_recv,
 ):
     axes, sections, rows_n, cols_n, factor, paired = dims
     micros, rows, cols, width = x_ref.shape
@@ -212,6 +212,15 @@
         left = pltpu.roll(field, 1, 1)
         right = pltpu.roll(field, pitch - 1, 1)
         return left.astype(BF16), field.astype(BF16), right.astype(BF16)
+
+    def out_store(m):
+        return pltpu.make_async_copy(out_ref.at[m], out_hbm.at[m], stores.at[m])
+
+    def grad_store(index):
+        rows_at = pl.ds(pl.multiple_of(index * chunk, 16), chunk)
+        return pltpu.make_async_copy(
+            fg_ref.at[rows_at], fg_hbm.at[rows_at], stores.at[micros + index]
+        )
 
     for m in range(micros):
         for d, dr, dc in around:
@@ -277,6 +286,7 @@
         tile = (pl.ds(2, rows), pl.ds(0, cols))
         masked = jnp.where(c2[tile] > 0, gf[(m, *tile)].astype(F32), 0.0)
         out_ref[m] = (masked + back.reshape(rows, cols, width)).astype(BF16)
+        out_store(m).start()
         for d, (dr, dc) in enumerate(SPREAD):
 
             @pl.when((s > 0) & inside(dr, dc))
@@ -348,15 +358,18 @@
             spread_copy(step).start()
         cross_copy(rows_n - 1).start()
         fg_ref[out_piece(c, r), :] = final[...].astype(F32)
+        grad_store(c * rows_n + r).start()
         for step in range(rows_n - 1):
             spread_copy(step).wait_recv()
             cross_copy(step).start()
             source = lax.rem(r + rows_n - step - 1, rows_n)
             fg_ref[out_piece(c, source), :] = gathered[step].astype(F32)
+            grad_store(c * rows_n + source).start()
         for step in [rows_n - 1, *range(rows_n - 1)]:
             cross_copy(step).wait_recv()
             source = lax.rem(r + 2 * rows_n - step - 1, rows_n)
             fg_ref[out_piece(1 - c, source), :] = crossed[step].astype(F32)
+            grad_store((1 - c) * rows_n + source).start()
         for step in range(rows_n - 1):
             sum_copy(step).wait_send()
             spread_copy(step).wait_send()
@@ -422,8 +435,12 @@
 
         each(group - 1, spread_out)
 
+        each(group, lambda step: grad_store(step).start())
         each(group - 1, lambda step: rs_copy(step).wait_send())
         each(group - 1, lambda step: ag_copy(step).wait_send())
+    each(group, lambda step: grad_store(step).wait())
+    for m in range(micros):
+        out_store(m).wait()
     for m in range(micros):
         for d, (dr, dc) in enumerate(SPREAD):
             if (dr, dc) != (0, 0):
@@ -454,11 +471,10 @@
     dims = (axes, sections, rows_n, cols_n, factor, paired)
     pitch = 2 * cols
     dma = pltpu.SemaphoreType.DMA
-    vmem = pl.BlockSpec(memory_space=pltpu.VMEM)
     field = pltpu.VMEM((micros, rows + 4, pitch, width), BF16)
     peers = max(group - 1, 1)
     wide = micros * rows * pitch if paired else pixels
-    hbm = pl.BlockSpec(memory_space=pltpu.HBM)
+    hbm = pl.BlockSpec(memory_space=pl.ANY)
     out, grads = pl.pallas_call(
         functools.partial(kernel, dims),
         out_shape=(
@@ -466,8 +482,10 @@
             jax.ShapeDtypeStruct((group * chunk, width), F32),
         ),
         in_specs=[hbm] * 7,
-        out_specs=(vmem, vmem),
+        out_specs=(hbm, hbm),
         scratch_shapes=[
+            pltpu.VMEM(out_grad.shape, BF16),
+            pltpu.VMEM((group * chunk, width), F32),
             field, field, field, field,
             pltpu.VMEM((2, 9, width, width), BF16),
             pltpu.VMEM((2, width), F32),
@@ -487,13 +505,13 @@
             pltpu.VMEM((peers, chunk, width), BF16),
             pltpu.VMEM((chunk, width), BF16),
             pltpu.VMEM((peers, chunk, width), BF16),
-            dma((7,)), dma((micros, 2)), dma((micros, 2)),
+            dma((micros + group,)), dma((7,)), dma((micros, 2)), dma((micros, 2)),
             dma((micros, 3, 9)), dma((micros, 3, 9)),
             dma((micros, 9)), dma((micros, 9)), dma((micros, 9)),
             dma((group + rows_n,)), dma((group + rows_n,)), dma((peers,)), dma((peers,)),
         ],
         compiler_params=pltpu.CompilerParams(
-            collective_id=0, has_side_effects=True, vmem_limit_bytes=40 * 1024 * 1024
+            collective_id=0, has_side_effects=True, vmem_limit_bytes=62 * 1024 * 1024
         ),
     )(
         section_input[0], first_pre[0], second_pre[0], out_grad,

time: 55.8 us -> 52.6 us (0.943)
  local copies, waits for them, and re-layouts: 7.41 us -> 3.86 us
  Pallas kernels: 47.3 us -> 47.9 us
    unnamed x16 -> x2, local copies, waits for them, and re-layouts: 7.41 us -> 3.86 us
    pallas_call x1, Pallas kernels: 47.3 us -> 47.9 us  [on_device(): pl.pallas_call(functools.partial(kernel, dims), out_shape=(jax.ShapeDtype...]
where the time goes in v3:
time: 52.6 us; the launch traced here: 52.4 us
  Pallas kernels  47.9 us (91%)
  local copies, waits for them, and re-layouts  3.86 us (7%)
  between operations  0.64 us (1%)
    pallas_call x1, Pallas kernels, on_device(): pl.pallas_call(functools.partial(kernel, dims), out_shape=(jax.ShapeDtype...  47.9 us
    unnamed x2, local copies, waits for them, and re-layouts  3.86 us

profile of v3, /device:TPU:0, one launch (start us, length us, event | category | flops | bytes accessed | tf_op | source)
XLA Modules:
  0.0 52.4 jit_solution(2055719665063767789)
XLA Ops:
  0.6 47.9 %shard_map.86 = (bf16[2,8,16,128]{3,2,1,0:T(8,128)(2,1)}, f32[2304,128]{1,0:T(8,128)}) custom-call(bf16[2,8,16,128]{3,2,1,0:T(8,128)(2,1)} %bitcast.11, bf16[2,8,16,128]{3,2,1,0:T(8,128)(2,1)} %bitcast.12, bf16[2,8,16,128]{3,2,1,0:T(8,128)(2,1)} %bitcast.13, bf16[2,8,16,128]{3,2,1,0:T(8,128)(2,1)} %og_ref.1, bf16[2,9,128,128]{3,2,1,0:T(8,128)(2,1)} %bitcast.9, ...), custom_call_target="tpu_custom_call" | custom-call | tf_op jit(solution)/shard_map/pallas_call | solution.py:478
  48.5 1.5 %copy.11 = bf16[1,2,8,16,128]{4,3,2,1,0:T(8,128)(2,1)} copy(bf16[1,2,8,16,128]{4,3,2,1,0:T(8,128)(2,1)} %bitcast.10) | data formatting | bytes 131072
  50.0 2.4 %copy.12 = f32[1,2,3,3,128,128]{5,4,3,2,1,0:T(8,128)} copy(f32[1,2,3,3,128,128]{5,4,3,2,1,0:T(8,128)} %bitcast.8) | data formatting | bytes 2359296

commit v4 on v3

--- a/solution.py
+++ b/solution.py
@@ -30,15 +30,15 @@
     dims, x_ref, p1_ref, p2_ref, og_ref, k_hbm, scale_hbm, shift_hbm,
     out_hbm, fg_hbm,
     out_ref, fg_ref, xf, p1f, p2f, gf, k_ref, scale_ref, shift_ref, kt, c1, c2, cols1, cols2, act,
-    union_x, union_g, spare_x, spare_g, crossed, red, inbox, final, gathered,
+    union_x, union_g, spare_x, spare_g, crossed, parted, red, inbox, final, gathered,
     stores, local, pair_send, pair_recv, halo_send, halo_recv, og_send, g_send, g_recv, rs_send, rs_recv, ag_send, ag_recv,
 ):
-    axes, sections, rows_n, cols_n, factor, paired = dims
+    axes, sections, rows_n, cols_n, factor, paired, chunk_rows = dims
     micros, rows, cols, width = x_ref.shape
     pitch = 2 * cols
     half = cols // 2
     group = rows_n * cols_n
-    chunk = final.shape[0]
+    chunk = chunk_rows
     s = lax.axis_index("section")
     r = lax.axis_index("row")
     c = lax.axis_index("col")
@@ -215,12 +215,6 @@
 
     def out_store(m):
         return pltpu.make_async_copy(out_ref.at[m], out_hbm.at[m], stores.at[m])
-
-    def grad_store(index):
-        rows_at = pl.ds(pl.multiple_of(index * chunk, 16), chunk)
-        return pltpu.make_async_copy(
-            fg_ref.at[rows_at], fg_hbm.at[rows_at], stores.at[micros + index]
-        )
 
     for m in range(micros):
         for d, dr, dc in around:
@@ -319,62 +313,76 @@
                 total[:, k * width : (k + 1) * width] * factor
             ).astype(BF16)
 
-        def row_piece(index):
-            return pl.ds(pl.multiple_of(index * chunk, 16), chunk)
-
-        def out_piece(conv, index):
-            return pl.ds(pl.multiple_of((conv * rows_n + index) * chunk, 16), chunk)
-
-        def row_copy(step, src, dst, send, recv):
-            peer = lax.rem(r + step + 1, rows_n)
+        parts = parted.shape[0]
+        sub = parted.shape[1]
+        side = lax.rem(r, 2)
+        beside = r + 1 - 2 * side
+        across = lax.rem(r + 2, 4)
+
+        def half_rows(which, q):
+            return pl.ds(pl.multiple_of((which * parts + q) * sub, 16), sub)
+
+        def send(src, dst, sem, where):
             return pltpu.make_async_remote_copy(
-                src_ref=red.at[row_piece(peer)] if src is red else src, dst_ref=dst.at[step],
-                send_sem=send.at[step], recv_sem=recv.at[step],
-                device_id=dev(s, peer, c), device_id_type=MESH,
-            )
-
-        def cross_copy(step):
-            return pltpu.make_async_remote_copy(
-                src_ref=gathered.at[step] if step < rows_n - 1 else final,
-                dst_ref=crossed.at[step],
-                send_sem=rs_send.at[rows_n + step], recv_sem=rs_recv.at[rows_n + step],
-                device_id=dev(s, r, 1 - c), device_id_type=MESH,
-            )
-
-        def sum_copy(step):
-            return row_copy(step, red, inbox, rs_send, rs_recv)
-
-        def spread_copy(step):
-            return row_copy(step, final, gathered, ag_send, ag_recv)
-
-        for step in range(rows_n - 1):
-            sum_copy(step).start()
-        summed = red[row_piece(r), :].astype(F32)
-        for step in range(rows_n - 1):
-            sum_copy(step).wait_recv()
-            summed = summed + inbox[step].astype(F32)
-        final[...] = summed.astype(BF16)
-        for step in range(rows_n - 1):
-            spread_copy(step).start()
-        cross_copy(rows_n - 1).start()
-        fg_ref[out_piece(c, r), :] = final[...].astype(F32)
-        grad_store(c * rows_n + r).start()
-        for step in range(rows_n - 1):
-            spread_copy(step).wait_recv()
-            cross_copy(step).start()
-            source = lax.rem(r + rows_n - step - 1, rows_n)
-            fg_ref[out_piece(c, source), :] = gathered[step].astype(F32)
-            grad_store(c * rows_n + source).start()
-        for step in [rows_n - 1, *range(rows_n - 1)]:
-            cross_copy(step).wait_recv()
-            source = lax.rem(r + 2 * rows_n - step - 1, rows_n)
-            fg_ref[out_piece(1 - c, source), :] = crossed[step].astype(F32)
-            grad_store((1 - c) * rows_n + source).start()
-        for step in range(rows_n - 1):
-            sum_copy(step).wait_send()
-            spread_copy(step).wait_send()
-        for step in range(rows_n):
-            cross_copy(step).wait_send()
+                src_ref=src, dst_ref=dst, send_sem=rs_send.at[sem], recv_sem=rs_recv.at[sem],
+                device_id=where, device_id_type=MESH,
+            )
+
+        def beside_sum(q):
+            return send(red.at[half_rows(1 - side, q)], inbox.at[q], q, dev(s, beside, c))
+
+        def across_sum(q):
+            return send(parted.at[q], inbox.at[parts + q], parts + q, dev(s, across, c))
+
+        def beside_copy(q):
+            return send(final.at[q], gathered.at[q], 2 * parts + q, dev(s, beside, c))
+
+        def cross_copy(q):
+            src = final.at[q] if q < parts else gathered.at[q - parts]
+            return send(src, crossed.at[q], 3 * parts + q, dev(s, r, 1 - c))
+
+        def grad_store(src, conv, which, q, slot):
+            rows_at = pl.ds(
+                pl.multiple_of(((conv * 2 + which) * parts + q) * sub, 16), sub
+            )
+            return pltpu.make_async_copy(src, fg_hbm.at[rows_at], stores.at[micros + slot])
+
+        written = []
+        for q in range(parts):
+            beside_sum(q).start()
+        for q in range(parts):
+            beside_sum(q).wait_recv()
+            parted[q] = (
+                red[half_rows(side, q), :].astype(F32) + inbox[q].astype(F32)
+            ).astype(BF16)
+            across_sum(q).start()
+        for q in range(parts):
+            across_sum(q).wait_recv()
+            final[q] = (parted[q].astype(F32) + inbox[parts + q].astype(F32)).astype(BF16)
+            beside_copy(q).start()
+            cross_copy(q).start()
+            written.append(grad_store(final.at[q], c, side, q, q))
+            written[-1].start()
+        for q in range(parts):
+            beside_copy(q).wait_recv()
+            cross_copy(parts + q).start()
+            written.append(grad_store(gathered.at[q], c, 1 - side, q, parts + q))
+            written[-1].start()
+        for q in range(2 * parts):
+            cross_copy(q).wait_recv()
+            which = side if q < parts else 1 - side
+            written.append(
+                grad_store(crossed.at[q], 1 - c, which, q % parts, 2 * parts + q)
+            )
+            written[-1].start()
+        for q in range(parts):
+            beside_sum(q).wait_send()
+            across_sum(q).wait_send()
+            beside_copy(q).wait_send()
+        for q in range(2 * parts):
+            cross_copy(q).wait_send()
+        for store in written:
+            store.wait()
         for m in range(micros):
             for which in range(2):
                 pair_copy(m, which, *pairs[which]).wait_send()
@@ -418,27 +426,33 @@
             )
 
         each(group - 1, lambda step: rs_copy(step).start())
-        fg_ref[piece(me), :] = red[piece(me), :].astype(F32)
+        fg_ref[...] = red[piece(me), :].astype(F32)
 
         def gather_in(step):
             rs_copy(step).wait_recv()
-            fg_ref[piece(me), :] += inbox[step].astype(F32)
+            fg_ref[...] += inbox[step].astype(F32)
 
         each(group - 1, gather_in)
-        final[...] = fg_ref[piece(me), :].astype(BF16)
+        final[...] = fg_ref[...].astype(BF16)
+
+        def grad_store(src, index, slot):
+            return pltpu.make_async_copy(
+                src, fg_hbm.at[piece(index)], stores.at[micros + slot]
+            )
+
+        grad_store(final, me, group - 1).start()
         each(group - 1, lambda step: ag_copy(step).start())
 
         def spread_out(step):
             ag_copy(step).wait_recv()
             source = lax.rem(me + group - step - 1, group)
-            fg_ref[piece(source), :] = gathered[step].astype(F32)
+            grad_store(gathered.at[step], source, step).start()
 
         each(group - 1, spread_out)
 
-        each(group, lambda step: grad_store(step).start())
+        each(group, lambda step: grad_store(final, me, step).wait())
         each(group - 1, lambda step: rs_copy(step).wait_send())
         each(group - 1, lambda step: ag_copy(step).wait_send())
-    each(group, lambda step: grad_store(step).wait())
     for m in range(micros):
         out_store(m).wait()
     for m in range(micros):
@@ -467,8 +481,10 @@
     chunk = 16 * (-(-tiles // group))
     pixels = micros * rows * cols
     factor = 1.0 / (pixels * group) ** 0.5
-    paired = cols_n == 2 and tiles % group == 0
-    dims = (axes, sections, rows_n, cols_n, factor, paired)
+    parts = 3
+    paired = cols_n == 2 and rows_n == 4 and tiles % (4 * parts) == 0
+    sub = 16 * tiles // (4 * parts) if paired else 16
+    dims = (axes, sections, rows_n, cols_n, factor, paired, chunk)
     pitch = 2 * cols
     dma = pltpu.SemaphoreType.DMA
     field = pltpu.VMEM((micros, rows + 4, pitch, width), BF16)
@@ -479,13 +495,13 @@
         functools.partial(kernel, dims),
         out_shape=(
             jax.ShapeDtypeStruct(out_grad.shape, BF16),
-            jax.ShapeDtypeStruct((group * chunk, width), F32),
+            jax.ShapeDtypeStruct((group * chunk, width), BF16),
         ),
         in_specs=[hbm] * 7,
         out_specs=(hbm, hbm),
         scratch_shapes=[
             pltpu.VMEM(out_grad.shape, BF16),
-            pltpu.VMEM((group * chunk, width), F32),
+            pltpu.VMEM((chunk, width), F32),
             field, field, field, field,
             pltpu.VMEM((2, 9, width, width), BF16),
             pltpu.VMEM((2, width), F32),
@@ -500,15 +516,16 @@
             pltpu.VMEM((micros, rows + 2, pitch, width), BF16),
             pltpu.VMEM((micros, rows, cols, width), BF16),
             pltpu.VMEM((micros, rows + 2, cols, width), BF16),
-            pltpu.VMEM((rows_n, chunk, width), BF16),
+            pltpu.VMEM((2 * parts, sub, width), BF16),
+            pltpu.VMEM((parts, sub, width), BF16),
             pltpu.VMEM((group * chunk, width), BF16),
-            pltpu.VMEM((peers, chunk, width), BF16),
-            pltpu.VMEM((chunk, width), BF16),
-            pltpu.VMEM((peers, chunk, width), BF16),
-            dma((micros + group,)), dma((7,)), dma((micros, 2)), dma((micros, 2)),
+            pltpu.VMEM((2 * parts, sub, width) if paired else (peers, chunk, width), BF16),
+            pltpu.VMEM((parts, sub, width) if paired else (chunk, width), BF16),
+            pltpu.VMEM((parts, sub, width) if paired else (peers, chunk, width), BF16),
+            dma((micros + max(group, 4 * parts),)), dma((7,)), dma((micros, 2)), dma((micros, 2)),
             dma((micros, 3, 9)), dma((micros, 3, 9)),
             dma((micros, 9)), dma((micros, 9)), dma((micros, 9)),
-            dma((group + rows_n,)), dma((group + rows_n,)), dma((peers,)), dma((peers,)),
+            dma((max(peers, 5 * parts),)), dma((max(peers, 5 * parts),)), dma((peers,)), dma((peers,)),
         ],
         compiler_params=pltpu.CompilerParams(
             collective_id=0, has_side_effects=True, vmem_limit_bytes=62 * 1024 * 1024
@@ -517,7 +534,7 @@
         section_input[0], first_pre[0], second_pre[0], out_grad,
         kernels[0].reshape(2, 9, width, width), bn_scale[0], bn_shift[0],
     )
-    grads = grads[: 18 * width].reshape(1, 2, 3, 3, width, width)
+    grads = grads[: 18 * width].astype(F32).reshape(1, 2, 3, 3, width, width)
     return out[None], grads
 
 

time: 52.6 us -> 50.7 us (0.964)
  local copies, waits for them, and re-layouts: 3.86 us -> 0.63 us
  other arithmetic: 0 us -> 2.24 us
  Pallas kernels: 47.9 us -> 47.1 us
    unnamed x2 -> x3, local copies, waits for them, and re-layouts: 3.86 us -> 0.63 us
    reshape x0 -> x1, other arithmetic: none -> 2.24 us  [on_device(): grads = grads[:18 * width].astype(F32).reshape(1, 2, 3, 3, width, width)]
    pallas_call x1, Pallas kernels: 47.9 us -> 47.1 us  [on_device(): pl.pallas_call(functools.partial(kernel, dims), out_shape=(jax.ShapeDtype...]
where the time goes in v4:
time: 50.7 us; the launch traced here: 50.6 us
  Pallas kernels  47.1 us (93%)
  other arithmetic  2.24 us (4%)
  between operations  0.65 us (1%)
  local copies, waits for them, and re-layouts  0.63 us (1%)
    pallas_call x1, Pallas kernels, on_device(): pl.pallas_call(functools.partial(kernel, dims), out_shape=(jax.ShapeDtype...  47.1 us
    reshape x1, other arithmetic, on_device(): grads = grads[:18 * width].astype(F32).reshape(1, 2, 3, 3, width, width)  2.24 us

profile of v4, /device:TPU:0, one launch (start us, length us, event | category | flops | bytes accessed | tf_op | source)
XLA Modules:
  0.0 50.6 jit_solution(13167252336763088735)
XLA Ops:
  0.6 47.1 %shard_map.86 = (bf16[2,8,16,128]{3,2,1,0:T(8,128)(2,1)}, bf16[2304,128]{1,0:T(8,128)(2,1)}) custom-call(bf16[2,8,16,128]{3,2,1,0:T(8,128)(2,1)} %bitcast.12, bf16[2,8,16,128]{3,2,1,0:T(8,128)(2,1)} %bitcast.13, bf16[2,8,16,128]{3,2,1,0:T(8,128)(2,1)} %bitcast.14, bf16[2,8,16,128]{3,2,1,0:T(8,128)(2,1)} %og_ref.1, bf16[2,9,128,128]{3,2,1,0:T(8,128)(2,1)} %bitcast.10, ...), custom_call_target="tpu_custom_call" | custom-call | tf_op jit(solution)/shard_map/pallas_call | solution.py:494
  47.7 0.0 copy-start
  47.7 2.2 %convert.1 = f32[1,2,3,3,128,128]{5,4,3,2,1,0:T(8,128)} convert(bf16[1,2,3,3,128,128]{5,4,3,2,1,0:T(8,128)(2,1)} %bitcast.9) | non-fusion elementwise | flops 294912 | bytes 1769472 | tf_op jit(solution)/shard_map/reshape | solution.py:537
  50.0 0.0 copy-done
  50.0 0.6 %copy.10 = bf16[1,2,8,16,128]{4,3,2,1,0:T(8,128)(2,1)} copy(bf16[1,2,8,16,128]{4,3,2,1,0:T(8,128)(2,1)S(1)} %bitcast.11) | data formatting | bytes 131072
Async XLA Ops:
  47.7 2.2 %copy-start = (bf16[2,8,16,128]{3,2,1,0:T(8,128)(2,1)S(1)}, bf16[2,8,16,128]{3,2,1,0:T(8,128)(2,1)}, u32[]{:S(2)}) copy-start(bf16[2,8,16,128]{3,2,1,0:T(8,128)(2,1)} %get-tuple-element.4) | copy-start | bytes 196612

commit v5 on v4

--- a/solution.py
+++ b/solution.py
@@ -304,10 +304,11 @@
                     cols2[
                         pl.ds(m * area, area), pl.ds((3 * i + j) * width, width)
                     ] = moved[j][i : i + rows].reshape(area, width)
-        total = lax.dot_general(
-            union_x[...].reshape(micros * area, width), cols2[...],
-            (((0,), (0,)), ((), ())), preferred_element_type=F32,
-        )
+            term = lax.dot_general(
+                union_x[m].reshape(area, width), cols2[pl.ds(m * area, area), :],
+                (((0,), (0,)), ((), ())), preferred_element_type=F32,
+            )
+            total = term if m == 0 else total + term
         for k in range(9):
             red[pl.ds((8 - k) * width, width), :] = (
                 total[:, k * width : (k + 1) * width] * factor

time: 50.7 us -> 50.4 us (level)
  no operation moved by 1% of the time
where the time goes in v5:
time: 50.4 us; the launch traced here: 50.2 us
  Pallas kernels  46.7 us (93%)
  other arithmetic  2.24 us (4%)
  between operations  0.65 us (1%)
  local copies, waits for them, and re-layouts  0.63 us (1%)
    pallas_call x1, Pallas kernels, on_device(): pl.pallas_call(functools.partial(kernel, dims), out_shape=(jax.ShapeDtype...  46.7 us
    reshape x1, other arithmetic, on_device(): grads = grads[:18 * width].astype(F32).reshape(1, 2, 3, 3, width, width)  2.24 us

profile of v5, /device:TPU:0, one launch (start us, length us, event | category | flops | bytes accessed | tf_op | source)
XLA Modules:
  0.0 50.2 jit_solution(12214147558182282991)
XLA Ops:
  0.6 46.7 %shard_map.86 = (bf16[2,8,16,128]{3,2,1,0:T(8,128)(2,1)}, bf16[2304,128]{1,0:T(8,128)(2,1)}) custom-call(bf16[2,8,16,128]{3,2,1,0:T(8,128)(2,1)} %bitcast.12, bf16[2,8,16,128]{3,2,1,0:T(8,128)(2,1)} %bitcast.13, bf16[2,8,16,128]{3,2,1,0:T(8,128)(2,1)} %bitcast.14, bf16[2,8,16,128]{3,2,1,0:T(8,128)(2,1)} %og_ref.1, bf16[2,9,128,128]{3,2,1,0:T(8,128)(2,1)} %bitcast.10, ...), custom_call_target="tpu_custom_call" | custom-call | tf_op jit(solution)/shard_map/pallas_call | solution.py:495
  47.4 0.0 copy-start
  47.4 2.2 %convert.1 = f32[1,2,3,3,128,128]{5,4,3,2,1,0:T(8,128)} convert(bf16[1,2,3,3,128,128]{5,4,3,2,1,0:T(8,128)(2,1)} %bitcast.9) | non-fusion elementwise | flops 294912 | bytes 1769472 | tf_op jit(solution)/shard_map/reshape | solution.py:538
  49.6 0.0 copy-done
  49.6 0.6 %copy.10 = bf16[1,2,8,16,128]{4,3,2,1,0:T(8,128)(2,1)} copy(bf16[1,2,8,16,128]{4,3,2,1,0:T(8,128)(2,1)S(1)} %bitcast.11) | data formatting | bytes 131072
Async XLA Ops:
  47.4 2.2 %copy-start = (bf16[2,8,16,128]{3,2,1,0:T(8,128)(2,1)S(1)}, bf16[2,8,16,128]{3,2,1,0:T(8,128)(2,1)}, u32[]{:S(2)}) copy-start(bf16[2,8,16,128]{3,2,1,0:T(8,128)(2,1)} %get-tuple-element.4) | copy-start | bytes 196612
